TPU v7x, 256 devices: a whole 4x4x8 slice. The times are simulated.
256 devices in a mesh: rows: 64 (over z, y, core), grp: 4 (over x).
Axes of the slice: x: 4, y: 4, z: 8, core: 2. Of those that a mesh axis runs over, the one named last changes fastest.
Arguments:
- matrix: float32 [524288, 512], P(('rows', 'grp')), may hold values from -6 to 6
- sign_bits: int32 [524288], P(('rows', 'grp')), may hold values from 0 to 1
- samples: int32 [16, 16384], P('grp'), may hold values from 0 to 32767, as said below
Outputs:
- r_factor: float32 [512, 512], replicated
- solved: float32 [524288, 512], P(('rows', 'grp'))
Inputs may be any that keep to these rules, and one draw needn't show every extreme that they name: `samples`: each row names 16384 distinct positions of a batch, exactly one of each pair 2 k and 2 k + 1, in any order.
All inputs are finite; a program needn't handle non-finite values.
Results may differ from a plain program's by a relative error of at most 0.0001.
Values sent between devices are 32-bit elements; how exact they have to be, the bound alone decides.
No kernel may reach another device: no remote copies, remote signals or barrier semaphores. Data moves between devices by JAX's collectives and lax.ppermute only.
A program may use at most 128 MiB of HBM per device.

v0:
```python
import jax
import jax.numpy as jnp
from jax import lax
from jax.sharding import PartitionSpec as P

INNER = 256


def cosine_sorted(size):
    evens = jnp.arange(0, size, 2, dtype=jnp.int32)
    odds = jnp.arange(1, size, 2, dtype=jnp.int32)
    freq = jnp.concatenate([evens, odds])[:, None]
    place = jnp.arange(size, dtype=jnp.int32)[None, :]
    phase = (2 * place + 1) * freq % (4 * size)
    weight = jnp.where(freq == 0, 1.0, 2.0).astype(jnp.float32) / size
    return jnp.sqrt(weight) * jnp.cos(jnp.pi * phase.astype(jnp.float32) / (2 * size))


def cosine(size):
    freq = jnp.arange(size, dtype=jnp.int32)[:, None]
    place = jnp.arange(size, dtype=jnp.int32)[None, :]
    phase = (2 * place + 1) * freq % (4 * size)
    weight = jnp.where(freq == 0, 1.0, 2.0).astype(jnp.float32) / size
    return jnp.sqrt(weight) * jnp.cos(jnp.pi * phase.astype(jnp.float32) / (2 * size))


def pair_parity(chosen):
    return jnp.zeros(chosen.shape, jnp.int32).at[chosen // 2].set(chosen % 2)


def local(matrix, sign_bits, samples):
    nrows = lax.axis_size("rows")
    ngroups = lax.axis_size("grp")
    batches, half = samples.shape
    per_device = matrix.shape[0] // batches
    width = matrix.shape[1]
    narrow = width // nrows
    total = per_device * nrows
    outer = total // INNER
    halfin = INNER // 2
    signed = matrix * (1 - 2 * sign_bits).astype(jnp.float32)[:, None]
    local_rows = signed.reshape(batches, per_device // INNER, INNER, width)
    c_inner = cosine_sorted(INNER)
    c_outer = cosine(outer)
    first = jnp.einsum("qp,bspn->bnsq", c_inner, local_rows, precision=lax.Precision.HIGHEST)
    first = first.reshape(batches, width, per_device)
    owned = lax.all_to_all(first, "rows", split_axis=1, concat_axis=2, tiled=True)
    mixed = jnp.einsum(
        "ap,bcpq->bcaq",
        c_outer,
        owned.reshape(batches, narrow, outer, INNER),
        precision=lax.Precision.HIGHEST,
    )
    parity = jax.vmap(pair_parity)(samples)
    even_rows = mixed[:, :, :, :halfin].reshape(batches, narrow, half)
    odd_rows = mixed[:, :, :, halfin:].reshape(batches, narrow, half)
    picked = jnp.where(parity[:, None, :] == 1, odd_rows, even_rows)
    rows_back = lax.all_to_all(picked, "rows", split_axis=2, concat_axis=1, tiled=True)
    gram = jnp.einsum("bnr,bmr->nm", rows_back, rows_back, precision=lax.Precision.HIGHEST)
    gram = lax.psum(gram, ("rows", "grp"))
    gram = gram / (ngroups * batches * half)
    lower = jnp.linalg.cholesky(gram)
    inverse = jax.scipy.linalg.solve_triangular(
        lower, jnp.eye(width, dtype=jnp.float32), lower=True
    )
    solved = jnp.dot(
        matrix, inverse.T, precision=lax.Precision.HIGHEST, preferred_element_type=jnp.float32
    )
    return (lower.T, solved)


def solution(mesh):
    placed = (P(("rows", "grp"), None), P(("rows", "grp")), P("grp", None))
    return jax.shard_map(
        local,
        mesh=mesh,
        in_specs=placed,
        out_specs=(P(), P(("rows", "grp"), None)),
        check_vma=False,
    )
```

profile of v0, /device:TPU:1, one launch (start us, length us, event | category | flops | bytes accessed | tf_op | source)
XLA Modules:
  0.0 941.1 jit_solution(5274258557876319001)
XLA Ops:
  7.9 2.5 broadcast_multiply_fusion
  10.5 7.6 fusion.30
  18.0 5.4 copy.18
  23.5 13.5 %all-to-all-start = ((f32[4,512,512]{2,0,1:T(4,128)}), f32[4,512,512]{2,0,1:T(4,128)}, u32[]{:S(2)}, u32[]{:S(2)}) async-start(f32[4,512,512]{2,0,1:T(4,128)} %copy.18), calls=%async_computation | async-start | bytes 8388608 | tf_op jit(solution)/shard_map/all_to_all | solution.py:47
  38.3 239.6 %scatter_custom_fusion = s32[65536]{0:T(1024)S(1)} fusion(s32[65536]{0:T(1024)S(1)} %bitcast.107, s32[65536]{0:T(1024)S(1)} %bitcast.108, s32[]{:T(128)} %copy.55), kind=kCustom, calls=%fused_computation.83 | custom fusion | bytes 262148
  278.0 3.5 copy.38
  281.5 4.4 copy.20
  286.0 5.2 reshape.110
  291.2 8.8 convolution_bitcast_fusion.1
  311.7 20.2 %copy.24 = f32[4,8,16384]{1,0,2:T(4,128)} copy(f32[4,8,16384]{2,1,0:T(8,128)S(1)} %broadcast_select_fusion) | data formatting | bytes 4194304 | tf_op jit(solution)/shard_map/jit(_where)/select_n | solution.py:57
  331.9 41.0 %reshape.149 = f32[64,1,8192]{2,1,0:T(1,128)S(1)} reshape(f32[16384,4,8]{2,1,0:T(4,128)} %bitcast.102) | data formatting | bytes 4194304
  372.9 60.4 %all_to_all.33 = f32[64,1,8192]{2,1,0:T(1,128)} all-to-all(f32[64,1,8192]{2,1,0:T(1,128)S(1)} %reshape.149), channel_id=1, replica_groups=mesh['rows'=64,'grp'=4] {'rows'}, dimensions={0} | all-to-all | bytes 4194304 | tf_op jit(solution)/shard_map/all_to_all | solution.py:58
  433.8 7.5 reduce.28
  441.4 41.6 %reshape.150 = f32[16384,4,8]{2,1,0:T(4,128)} reshape(f32[64,8192]{1,0:T(8,128)S(1)} %reduce.28) | data formatting | bytes 4194304
  483.0 23.7 %copy.25 = f32[4,8,64,256]{3,1,2,0:T(8,128)S(1)} copy(f32[4,8,64,256]{1,0,3,2:T(4,128)} %bitcast.103) | data formatting | bytes 4194304 | tf_op jit(solution)/shard_map/all_to_all | solution.py:58
  506.7 4.5 fusion.2
  512.4 254.0 %all-reduce.3.cloned.1.call-done = f32[512,512]{0,1:T(8,128)} async-done(((f32[512,512]{0,1:T(8,128)}), f32[512,512]{0,1:T(8,128)}) %all-reduce.3.cloned.1.call-update) | async-done | bytes 1048592 | tf_op jit(solution)/shard_map/psum | solution.py:60
  769.4 11.7 %cholesky.104 = f32[128,128]{1,0:T(8,128)S(1)} custom-call(f32[128,128]{1,0:T(8,128)S(1)} %cholesky.266), custom_call_target="Cholesky" | custom-call | tf_op jit(solution)/shard_map/jit(cholesky)/cholesky | solution.py:62
  781.1 9.8 %custom-call.31 = f32[1,128,128]{1,2,0:T(8,128)S(1)} custom-call(f32[1,128,128]{2,1,0:T(8,128)S(1)} %get-tuple-element.41), custom_call_target="InvertDiagBlocksLowerTriangular" | custom-call | tf_op jit(solution)/shard_map/jit(cholesky)/cholesky | solution.py:62
  793.7 11.9 %cholesky.217 = f32[128,128]{1,0:T(8,128)S(1)} custom-call(f32[128,128]{1,0:T(8,128)S(1)} %cholesky.270), custom_call_target="Cholesky" | custom-call | tf_op jit(solution)/shard_map/jit(cholesky)/cholesky | solution.py:62
  807.0 9.8 %custom-call.32 = f32[1,128,128]{1,2,0:T(8,128)S(1)} custom-call(f32[1,128,128]{2,1,0:T(8,128)S(1)} %get-tuple-element.38), custom_call_target="InvertDiagBlocksLowerTriangular" | custom-call | tf_op jit(solution)/shard_map/jit(cholesky)/cholesky | solution.py:62
  818.3 11.7 %cholesky.238 = f32[128,128]{1,0:T(8,128)S(1)} custom-call(f32[128,128]{1,0:T(8,128)S(1)} %cholesky.275), custom_call_target="Cholesky" | custom-call | tf_op jit(solution)/shard_map/jit(cholesky)/cholesky | solution.py:62
  830.8 9.8 %custom-call.33 = f32[1,128,128]{1,2,0:T(8,128)S(1)} custom-call(f32[1,128,128]{2,1,0:T(8,128)S(1)} %get-tuple-element.35), custom_call_target="InvertDiagBlocksLowerTriangular" | custom-call | tf_op jit(solution)/shard_map/jit(cholesky)/cholesky | solution.py:62
  842.4 11.7 %cholesky.255 = f32[128,128]{1,0:T(8,128)S(1)} custom-call(f32[128,128]{1,0:T(8,128)S(1)} %convolution_subtract_fusion.5), custom_call_target="Cholesky" | custom-call | tf_op jit(solution)/shard_map/jit(cholesky)/cholesky | solution.py:62
  858.6 14.1 %while.1 = (s32[]{:T(128)}, f32[512,512]{1,0:T(8,128)}, s32[4,2]{0,1:T(2,128)S(1)}, f32[4,128,128]{2,1,0:T(8,128)}, s32[]{:T(128)}) while((s32[]{:T(128)}, f32[512,512]{1,0:T(8,128)}, s32[4,2]{0,1:T(2,128)S(1)}, f32[4,128,128]{2,1,0:T(8,128)}, s32[]{:T(128)}) %tuple.37), condition=%wide.while_cond, body=%wide.while_body.sunk | while | flops 2 | bytes 132705 | solution.py:63
  859.3 2.9 bitcast_dynamic-update-slice_fusion.2
  862.8 2.9 bitcast_dynamic-update-slice_fusion.2
  866.3 2.9 bitcast_dynamic-update-slice_fusion.2
  869.9 2.8 bitcast_dynamic-update-slice_fusion.2
  872.7 40.1 %custom-call.34 = f32[4,128,128]{1,2,0:T(8,128)S(1)} custom-call(f32[4,128,128]{2,1,0:T(8,128)} %get-tuple-element.9), custom_call_target="InvertDiagBlocksLowerTriangular" | custom-call | tf_op jit(solution)/shard_map/jit(_solve_triangular)/triangular_solve | solution.py:63
  918.8 8.7 convolution_bitcast_fusion
  927.5 5.3 copy.29
  (82 shorter events, 38.5 us)
Async XLA Ops:
  23.5 13.5 %copy-start.4 = (s32[4,16384]{1,0:T(4,128)S(1)}, s32[4,16384]{1,0:T(4,128)}, u32[]{:S(2)}) copy-start(s32[4,16384]{1,0:T(4,128)} %param.5) | copy-start | bytes 786436
  23.5 14.1 %copy-start.5 = (s32[2]{0:T(128)S(1)}, s32[2]{0:T(128)}, u32[]{:S(2)}) copy-start(s32[2]{0:T(128)} %constant.238) | copy-start | bytes 28
  23.5 14.3 %copy-start.6 = (s32[2]{0:T(128)S(1)}, s32[2]{0:T(128)}, u32[]{:S(2)}) copy-start(s32[2]{0:T(128)} %constant.241) | copy-start | bytes 28
  23.5 254.5 %all-to-all-start = ((f32[4,512,512]{2,0,1:T(4,128)}), f32[4,512,512]{2,0,1:T(4,128)}, u32[]{:S(2)}, u32[]{:S(2)}) async-start(f32[4,512,512]{2,0,1:T(4,128)} %copy.18), calls=%async_computation | async-start | bytes 8388608 | tf_op jit(solution)/shard_map/all_to_all | solution.py:47
  37.0 729.4 %all-reduce.3.cloned.1.call-start = ((), (), s32[]{:S(2)}) async-start(), calls=%async_computation.2 | async-start | bytes 2097152 | tf_op jit(solution)/shard_map/psum | solution.py:60
  766.4 1.8 copy-start.1
  768.4 1.0 copy-start.3
  791.0 122.1 %copy-start.2 = (f32[512,512]{1,0:T(8,128)S(1)}, f32[512,512]{1,0:T(8,128)}, u32[]{:S(2)}) copy-start(f32[512,512]{1,0:T(8,128)} %fusion.23) | copy-start | bytes 3145732
  912.8 5.9 copy-start
Sparse Core Ops, SparseCore 0:
  511.3 255.0 all-reduce.2
where the time goes:
time: 951 us; the launch traced here: 941 us
  local copies, waits for them, and re-layouts  417 us (44%)
  waiting for transfers between devices  254 us (27%)
  other arithmetic  138 us (15%)
  blocking collectives  60.4 us (6%)
  matrix products  41.3 us (4%)
  between operations  17.2 us (2%)
  starting transfers between devices  13.5 us (1%)
    unnamed x22, local copies, waits for them, and re-layouts  330 us
    psum x1, waiting for transfers between devices, local(): gram = lax.psum(gram, ('rows', 'grp'))  254 us
    another operation x15, other arithmetic, local(): lower = jnp.linalg.cholesky(gram)  79.3 us
    all_to_all x1, blocking collectives, local(): lax.all_to_all(picked, 'rows', split_axis=2, concat_axis=1, tiled=True)  60.4 us
    another operation x3, other arithmetic, local(): jax.scipy.linalg.solve_triangular(lower, jnp.eye(width, dtype=jnp.float32...  41.4 us
    all_to_all x2, local copies, waits for them, and re-layouts, local(): lax.all_to_all(picked, 'rows', split_axis=2, concat_axis=1, tiled=True)  24.2 us
    select_n x1, local copies, waits for them, and re-layouts, local(): picked = jnp.where(parity[:, None, :] == 1, odd_rows, even_rows)  20.2 us
  transfers between devices with their start and end apart: 2, of which 1 were waited for; matrix products, arithmetic and copies ran while one was open for 26% of the time, Pallas kernels for 0%

commit v1 on v0

v1 whole, which is shorter than its diff:
```python
import functools
import numpy as np
import jax
import jax.numpy as jnp
from jax import lax
from jax.sharding import Mesh
from jax.sharding import PartitionSpec as P
from jax.experimental import pallas as pl
from jax.experimental.pallas import tpu as pltpu

F32, BF16 = jnp.float32, jnp.bfloat16
NT = (((1,), (1,)), ((), ()))
TN = (((0,), (0,)), ((), ()))


def cosine64(size):
    freq = np.arange(size)[:, None]
    place = np.arange(size)[None, :]
    weight = np.where(freq == 0, 1.0, 2.0) / size
    return np.sqrt(weight) * np.cos(np.pi * ((2 * place + 1) * freq % (4 * size)) / (2 * size))


def two(table):
    high = table.astype(np.float32).astype(jnp.bfloat16)
    low = (table - high.astype(np.float64)).astype(np.float32).astype(jnp.bfloat16)
    return high, low


def inner_tables():
    table = cosine64(256)
    swapped = table.reshape(32, 2, 4, 256)[:, ::-1].reshape(256, 256)
    return two(np.stack([table, swapped]))


def outer_tables():
    table = cosine64(128).reshape(128, 64, 2)
    both = np.stack([table, table[:, :, ::-1]])
    wide = np.broadcast_to(both[:, None, :, :, :, None], (2, 2, 128, 64, 2, 4))
    return two(wide.reshape(2, 256, 512))


def split(x):
    high = x.astype(BF16)
    return high, (x - high.astype(F32)).astype(BF16)


def dot(a, b, dims=(((1,), (0,)), ((), ()))):
    return lax.dot_general(a, b, dims, preferred_element_type=F32)


def inner_kernel(sign_ref, high_ref, low_ref, x_ref, out_ref):
    results = []
    for s in range(2):
        place = 4 * pl.program_id(0) + 2 * s
        bits = jnp.concatenate([sign_ref[pl.ds(place, 1), :], sign_ref[pl.ds(place + 1, 1), :]], axis=1)
        sign = (1 - 2 * bits).astype(F32).astype(BF16)
        ch, cl = high_ref[s] * sign, low_ref[s] * sign
        xh, xl = split(x_ref[s * 256 : (s + 1) * 256, :])
        results.append((dot(ch, xh) + (dot(cl, xh) + dot(ch, xl))).reshape(32, 8, 512))
    first, second = results
    upper = lax.broadcasted_iota(jnp.int32, first.shape, 1) < 4
    out_ref[:, 0, 0] = jnp.where(upper, first, second)
    out_ref[:, 1, 0] = jnp.where(upper, second, first)


def inner(matrix, sign_bits):
    batches = matrix.shape[0] // 512
    high, low = inner_tables()
    whole = pl.BlockSpec((2, 256, 256), lambda b: (0, 0, 0))
    return pl.pallas_call(
        inner_kernel,
        grid=(batches,),
        in_specs=[
            pl.BlockSpec((4 * batches, 128), lambda b: (0, 0)),
            whole,
            whole,
            pl.BlockSpec((512, 512), lambda b: (b, 0)),
        ],
        out_specs=pl.BlockSpec((32, 2, 1, 8, 512), lambda b: (0, 0, b, 0, 0)),
        out_shape=jax.ShapeDtypeStruct((32, 2, batches, 8, 512), F32),
        name="inner",
    )(sign_bits.reshape(4 * batches, 128), jnp.asarray(high), jnp.asarray(low), matrix)


def parity_kernel(first_ref, samples_ref, out_ref):
    batches, half = samples_ref.shape[0], samples_ref.shape[1]
    first = first_ref[0]
    step = 2048
    for b in range(batches):
        total = jnp.zeros((8, 128), F32)
        for start in range(0, half, step):
            pos = samples_ref[b : b + 1, start : start + step]
            a = lax.shift_right_logical(pos, 8)
            pair = lax.shift_right_logical(lax.bitwise_and(pos, 255), 1) - first
            odd = lax.bitwise_and(pos, 1)
            rows = lax.broadcasted_iota(jnp.int32, (128, step), 0)
            hot = (rows == a).astype(F32).astype(BF16)
            which = lax.broadcasted_iota(jnp.int32, (8, step), 0)
            mine = jnp.where(which == pair, odd, 0).astype(F32).astype(BF16)
            total = total + dot(mine, hot, NT)
        out_ref[b] = total


def parity(samples, first_pair):
    batches, half = samples.shape
    return pl.pallas_call(
        parity_kernel,
        grid_spec=pltpu.PrefetchScalarGridSpec(
            num_scalar_prefetch=1,
            grid=(1,),
            in_specs=[pl.BlockSpec((batches, half), lambda i, f: (0, 0))],
            out_specs=pl.BlockSpec((batches, 8, 128), lambda i, f: (0, 0, 0)),
        ),
        out_shape=jax.ShapeDtypeStruct((batches, 8, 128), F32),
        cost_estimate=pl.CostEstimate(flops=2 * batches * half * 128 * 8, bytes_accessed=4 * batches * half, transcendentals=0),
        name="parity",
    )(first_pair, samples)


def outer_kernel(scale, steps, par_ref, odd_ref, high_ref, low_ref, z_ref, keep_ref, send_ref, acc_ref):
    step = pl.program_id(0)
    z = z_ref[:, 0].reshape(512, 512)
    zh, zl = split(z)
    row = lax.broadcasted_iota(jnp.int32, (256, 512), 0)
    col = lax.broadcasted_iota(jnp.int32, (256, 512), 1)
    choice = 2 * lax.shift_right_logical(row, 7) + odd_ref[0].astype(jnp.int32)
    keep = jnp.where(lax.bitwise_and(col, 3) == choice, 1.0, 0.0).astype(BF16)
    wh, wl = high_ref[0] * keep, low_ref[0] * keep
    rows = dot(wh, zh) + (dot(wl, zh) + dot(wh, zl))
    rh, rl = split(rows)
    part = dot(rh, rh, TN) + (dot(rh, rl, TN) + dot(rl, rh, TN))

    @pl.when(step == 0)
    def _():
        acc_ref[...] = part

    @pl.when(step > 0)
    def _():
        acc_ref[...] += part

    @pl.when(step == steps - 1)
    def _():
        mine = pl.multiple_of(256 * par_ref[0], 256)
        keep_ref[...] = acc_ref[pl.ds(mine, 256), :] * scale
        send_ref[...] = acc_ref[pl.ds(256 - mine, 256), :] * scale


def outer(mixed, odd, par, scale):
    batches = mixed.shape[1]
    high, low = outer_tables()
    table = pl.BlockSpec((1, 256, 512), lambda b, p: (p[0], 0, 0))
    return pl.pallas_call(
        functools.partial(outer_kernel, scale, batches),
        grid_spec=pltpu.PrefetchScalarGridSpec(
            num_scalar_prefetch=1,
            grid=(batches,),
            in_specs=[
                pl.BlockSpec((1, 256, 1), lambda b, p: (b, 0, 0)),
                table,
                table,
                pl.BlockSpec((64, 1, 8, 512), lambda b, p: (0, b, 0, 0)),
            ],
            out_specs=[pl.BlockSpec((256, 512), lambda b, p: (0, 0))] * 2,
            scratch_shapes=[pltpu.VMEM((512, 512), F32)],
        ),
        out_shape=[jax.ShapeDtypeStruct((256, 512), F32)] * 2,
        name="outer",
    )(par, odd, jnp.asarray(high), jnp.asarray(low), mixed)


def hdot(a, b, dims=(((1,), (0,)), ((), ()))):
    return lax.dot_general(a, b, dims, precision=lax.Precision.HIGHEST, preferred_element_type=F32)


def factor(block):
    size = block.shape[0]
    lane = lax.broadcasted_iota(jnp.int32, (1, size), 1)
    groups = [block[8 * i : 8 * i + 8] for i in range(size // 8)]
    sub = lax.broadcasted_iota(jnp.int32, (8, size), 0)
    pivots = jnp.zeros((1, size), F32)
    pivot_rows = []
    for j in range(size):
        g, r = j // 8, j % 8
        row = groups[g][r : r + 1]
        pivot = row[:, j : j + 1]
        inverse = 1.0 / pivot
        row = jnp.where(lane == j, 1.0, row) * inverse
        pivot_rows.append(pivot)
        for i in range(g, size // 8):
            if i == g and r == 7:
                continue
            column = groups[i][:, j : j + 1]
            if i == g:
                column = jnp.where(sub[:, :1] > r, column, 0.0)
                rest = jnp.where((lane == j) & (sub > r), 0.0, groups[i])
            else:
                rest = jnp.where(lane == j, 0.0, groups[i])
            groups[i] = rest - column * row
    return jnp.concatenate(groups, axis=0), jnp.concatenate(pivot_rows, axis=0)


def solve_kernel(par_ref, own_ref, other_ref, x_ref, r_ref, out_ref, g_ref, inv_ref, xh_ref, xl_ref):
    n, nb = 512, 128
    mine = pl.multiple_of(256 * par_ref[0], 256)
    g_ref[pl.ds(mine, 256), :] = own_ref[...]
    g_ref[pl.ds(256 - mine, 256), :] = other_ref[...]
    inv_ref[...] = jnp.zeros((n, n), F32)
    r_ref[...] = jnp.zeros((n, n), F32)
    xh, xl = split(x_ref[...])
    xh_ref[...] = xh
    xl_ref[...] = xl
    row = lax.broadcasted_iota(jnp.int32, (nb, nb), 0)
    col = lax.broadcasted_iota(jnp.int32, (nb, nb), 1)
    for k in range(n // nb):
        lo, hi = k * nb, (k + 1) * nb
        m, pivots = factor(g_ref[lo:hi, lo:hi])
        root = lax.rsqrt(pivots)
        root = root * (1.5 - 0.5 * pivots * root * root)
        upper = jnp.where(col > row, m, jnp.where(col == row, pivots, 0.0)) * root
        linv = jnp.where(col < row, m, jnp.where(col == row, 1.0, 0.0)) * root
        r_ref[lo:hi, lo:hi] = upper
        rinv = linv.T
        inv_ref[lo:hi, lo:hi] = rinv
        if k + 1 < n // nb:
            panel = hdot(linv, g_ref[lo:hi, hi:])
            r_ref[lo:hi, hi:] = panel
            g_ref[hi:, hi:] -= hdot(panel, panel, TN)
        if k > 0:
            t = hdot(inv_ref[:lo, :lo], r_ref[:lo, lo:hi])
            inv_ref[:lo, lo:hi] = -hdot(t, rinv)
        ih, il = split(inv_ref[:hi, lo:hi])
        a, b = xh_ref[:, :hi], xl_ref[:, :hi]
        out_ref[:, lo:hi] = dot(a, ih) + (dot(b, ih) + dot(a, il))


def solve(par, own, other, matrix):
    rows, n = matrix.shape
    vmem = pl.BlockSpec(memory_space=pltpu.VMEM)
    smem = pl.BlockSpec(memory_space=pltpu.SMEM)
    return pl.pallas_call(
        solve_kernel,
        in_specs=[smem, vmem, vmem, vmem],
        out_specs=(vmem, vmem),
        out_shape=(jax.ShapeDtypeStruct((n, n), F32), jax.ShapeDtypeStruct((rows, n), F32)),
        scratch_shapes=[
            pltpu.VMEM((n, n), F32),
            pltpu.VMEM((n, n), F32),
            pltpu.VMEM((rows, n), BF16),
            pltpu.VMEM((rows, n), BF16),
        ],
        compiler_params=pltpu.CompilerParams(vmem_limit_bytes=48 * 2**20),
        name="solve",
    )(par, own, other, matrix)


def exchange(x, axes):
    return lax.all_to_all(x, axes, split_axis=0, concat_axis=0, tiled=True)


def spread(x, copies, axes):
    return exchange(jnp.broadcast_to(x[None], (copies,) + x.shape), axes)


def local(matrix, sign_bits, samples):
    batches, half = samples.shape
    core = lax.axis_index("core").astype(jnp.int32)
    device = lax.axis_index(("z", "y", "core")).astype(jnp.int32)
    par = core.reshape(1)
    sent = inner(matrix, sign_bits).reshape(64, batches, 8, 512)
    mixed = exchange(sent, ("z", "y", "core"))
    odd = parity(samples, (2 * device).reshape(1))[:, :2].reshape(batches, 256, 1)
    keep, send = outer(mixed, odd, par, 1.0 / (4 * batches * half))
    swap = [(0, 1), (1, 0)]
    part = keep + lax.ppermute(send, "core", swap)
    part = exchange(part.reshape(16, 16, 512), ("y", "x")).sum(0)
    part = spread(part, 8, "z").sum(0)
    own = spread(part, 16, ("y", "x")).reshape(256, 512)
    other = lax.ppermute(own, "core", swap)
    return solve(par, own, other, matrix)


def solution(mesh):
    parts = Mesh(mesh.devices.reshape(8, 4, 2, 4), ("z", "y", "core", "x"))
    every = ("z", "y", "core", "x")
    return jax.shard_map(
        local,
        mesh=parts,
        in_specs=(P(every, None), P(every), P("x", None)),
        out_specs=(P(), P(every, None)),
        check_vma=False,
    )
```

time: 951 us -> 229 us (0.24)
  local copies, waits for them, and re-layouts: 417 us -> 4.12 us
  waiting for transfers between devices: 254 us -> 90.1 us
  other arithmetic: 138 us -> 1.18 us
  Pallas kernels: 0 us -> 71 us
  matrix products: 41.3 us -> 0 us
  blocking collectives: 60.4 us -> 42 us
  between operations: 17.2 us -> 0.68 us
    unnamed x22 -> x2, local copies, waits for them, and re-layouts: 330 us -> 2.19 us
    psum x1 -> x0, waiting for transfers between devices: 254 us -> none  [local(): gram = lax.psum(gram, ('rows', 'grp'))]
    another operation x18 -> x0, other arithmetic: 121 us -> none  [the longest x15 79.3 us: local(): lower = jnp.linalg.cholesky(gram)]
    all_to_all x1, waiting for transfers between devices: 0.01 us -> 86.9 us  [exchange(): return lax.all_to_all(x, axes, split_axis=0, concat_axis=0, tiled=True)]
    pallas_call x0 -> x4, Pallas kernels: none -> 71 us  [the longest x1 51.2 us: solve(): pl.pallas_call(solve_kernel, in_specs=[smem, vmem, vmem, vmem], out_specs...]
    all_to_all x4 -> x0, local copies, waits for them, and re-layouts: 32.2 us -> none  [the longest x2 24.2 us: local(): lax.all_to_all(picked, 'rows', split_axis=2, concat_axis=1, tiled=True)]
    dot_general x4 -> x0, matrix products: 29.5 us -> none  [the longest x1 8.78 us: local(): jnp.einsum('ap,bcpq->bcaq', c_outer, owned.reshape(batches, narrow, outer...]
    select_n x1 -> x0, local copies, waits for them, and re-layouts: 20.2 us -> none  [local(): picked = jnp.where(parity[:, None, :] == 1, odd_rows, even_rows)]
  transfers between devices with their start and end apart: 2 -> 3, of which waited for: 1 -> 3; matrix products, arithmetic and copies ran while one was open for 26% -> 1% of each run, Pallas kernels for 0% -> 3%
where the time goes in v1:
time: 229 us; the launch traced here: 228 us
  waiting for transfers between devices  90.1 us (39%)
  Pallas kernels  71 us (31%)
  blocking collectives  42 us (18%)
  starting transfers between devices  19.3 us (8%)
  local copies, waits for them, and re-layouts  4.12 us (2%)
    all_to_all x1, waiting for transfers between devices, exchange(): return lax.all_to_all(x, axes, split_axis=0, concat_axis=0, tiled=True)  86.9 us
    pallas_call x1, Pallas kernels, solve(): pl.pallas_call(solve_kernel, in_specs=[smem, vmem, vmem, vmem], out_specs...  51.2 us
    all_to_all x3, blocking collectives, exchange(): return lax.all_to_all(x, axes, split_axis=0, concat_axis=0, tiled=True)  42 us
    all_to_all x1, starting transfers between devices, exchange(): return lax.all_to_all(x, axes, split_axis=0, concat_axis=0, tiled=True)  13.3 us
    pallas_call x1, Pallas kernels, outer(): pl.pallas_call(functools.partial(outer_kernel, scale, batches), grid_spec...  7.84 us
    pallas_call x1, Pallas kernels, parity(): pl.pallas_call(parity_kernel, grid_spec=pltpu.PrefetchScalarGridSpec(num_...  5.99 us
    pallas_call x1, Pallas kernels, inner(): pl.pallas_call(inner_kernel, grid=(batches,), in_specs=[pl.BlockSpec((4 *...  5.99 us
  transfers between devices with their start and end apart: 3, of which 3 were waited for; matrix products, arithmetic and copies ran while one was open for 1% of the time, Pallas kernels for 3%

profile of v1, /device:TPU:1, one launch (start us, length us, event | category | flops | bytes accessed | tf_op | source)
XLA Modules:
  0.0 228.4 jit_solution(7407280358847625322)
XLA Ops:
  0.6 6.0 %inner.1 = f32[32,2,4,8,512]{4,3,2,1,0:T(8,128)} custom-call(s32[16,128]{1,0:T(8,128)} %bitcast.10, bf16[2,256,256]{2,1,0:T(8,128)(2,1)} %constant.29.clone.high_ref, bf16[2,256,256]{2,1,0:T(8,128)(2,1)} %constant.30.clone.low_ref, f32[2048,512]{1,0:T(8,128)} %x_ref.3), custom_call_target="tpu_custom_call" | custom-call | tf_op jit(solution)/shard_map/inner/pallas_call | solution.py:70
  6.6 13.3 %all-to-all-start = ((f32[64,4,8,512]{3,2,1,0:T(8,128)}), f32[64,4,8,512]{3,2,1,0:T(8,128)}, u32[]{:S(2)}, u32[]{:S(2)}) async-start(f32[64,4,8,512]{3,2,1,0:T(8,128)} %bitcast.8), calls=%async_computation | async-start | bytes 8388608 | tf_op jit(solution)/shard_map/all_to_all | solution.py:257
  19.9 6.0 %parity.1 = f32[4,8,128]{2,1,0:T(8,128)} custom-call(s32[1]{0:T(128)} %bitcast.1.first_ref, s32[4,16384]{1,0:T(4,128)} %samples_ref.1), custom_call_target="tpu_custom_call" | custom-call | flops 134217728 | bytes 262144 | tf_op jit(solution)/shard_map/parity/pallas_call | solution.py:106
  25.9 0.7 slice.4
  26.6 1.1 reshape.34.odd_ref
  27.8 86.9 %all-to-all-done.z_ref = f32[64,4,8,512]{3,2,1,0:T(8,128)} async-done(((f32[64,4,8,512]{3,2,1,0:T(8,128)}), f32[64,4,8,512]{3,2,1,0:T(8,128)}, u32[]{:S(2)}, u32[]{:S(2)}) %all-to-all-start) | async-done | bytes 4194336 | tf_op jit(solution)/shard_map/all_to_all | solution.py:257
  114.6 7.8 %outer.1 = (f32[256,512]{1,0:T(8,128)}, f32[256,512]{1,0:T(8,128)}) custom-call(s32[1]{0:T(128)} %bitcast.par_ref, f32[4,256,1]{2,1,0:T(8,128)} %reshape.34.odd_ref, bf16[2,256,512]{2,1,0:T(8,128)(2,1)} %constant.31.clone.high_ref, bf16[2,256,512]{2,1,0:T(8,128)(2,1)} %constant.32.clone.low_ref, f32[64,4,8,512]{3,2,1,0:T(8,128)} %all-to-all-done.z_ref), custom_call_target="tpu_custom_call" | custom-call | tf_op jit(solution)/shard_map/outer/pallas_call | solution.py:152
  122.5 2.1 collective-permute-start
  124.5 1.7 collective-permute-done
  126.3 1.1 add.11
  127.4 17.0 %all_to_all.20 = f32[16,16,512]{2,1,0:T(8,128)S(1)} all-to-all(f32[16,16,512]{2,1,0:T(8,128)S(1)} %bitcast.9), channel_id=1, replica_groups=mesh['z'=8,'y'=4,'core'=2,'x'=4] {'y','x'}, dimensions={0} | all-to-all | bytes 1048576 | tf_op jit(solution)/shard_map/all_to_all | solution.py:257
  144.5 12.1 %all_to_all.21 = f32[8,16,512]{2,1,0:T(8,128)S(1)} all-to-all(f32[8,16,512]{2,1,0:T(8,128)S(1)} %broadcast_in_dim.4), channel_id=1, replica_groups=mesh['z'=8,'y'=4,'core'=2,'x'=4] {'z'}, dimensions={0} | all-to-all | bytes 524288 | tf_op jit(solution)/shard_map/all_to_all | solution.py:257
  156.6 0.1 broadcast_in_dim.5
  156.7 12.9 %all_to_all.22 = f32[16,16,512]{2,1,0:T(8,128)S(1)} all-to-all(f32[16,16,512]{2,1,0:T(8,128)S(1)} %broadcast_in_dim.5), channel_id=1, replica_groups=mesh['z'=8,'y'=4,'core'=2,'x'=4] {'y','x'}, dimensions={0} | all-to-all | bytes 1048576 | tf_op jit(solution)/shard_map/all_to_all | solution.py:257
  169.6 3.9 %collective-permute-start.1 = (f32[256,512]{1,0:T(8,128)S(1)}, f32[256,512]{1,0:T(8,128)S(1)}, u32[]{:S(2)}, u32[]{:S(2)}) collective-permute-start(f32[256,512]{1,0:T(8,128)S(1)} %bitcast.6), channel_id=1, source_target_pairs={{0,4},{4,0},{1,5},{5,1},{2,6},{6,2},{3,7},{7,3},{8,12},{12,8},{9,1... | collective-permute-start | bytes 1572872 | tf_op jit(solution)/shard_map/ppermute | solution.py:278
  173.5 1.5 collective-permute-done.1.other_ref
  175.0 0.0 copy-start
  175.0 2.2 copy-done
  177.2 51.2 %solve.1 = (f32[512,512]{1,0:T(8,128)}, f32[2048,512]{1,0:T(8,128)}) custom-call(s32[1]{0:T(128)} %bitcast.par_ref, f32[256,512]{1,0:T(8,128)S(1)} %bitcast.7, f32[256,512]{1,0:T(8,128)S(1)} %collective-permute-done.1.other_ref, f32[2048,512]{1,0:T(8,128)S(1)} %copy-done), custom_call_target="tpu_custom_call" | custom-call | tf_op jit(solution)/shard_map/solve/pallas_call | solution.py:240
  (3 shorter events, 0.1 us)
Async XLA Ops:
  6.6 108.0 %all-to-all-start = ((f32[64,4,8,512]{3,2,1,0:T(8,128)}), f32[64,4,8,512]{3,2,1,0:T(8,128)}, u32[]{:S(2)}, u32[]{:S(2)}) async-start(f32[64,4,8,512]{3,2,1,0:T(8,128)} %bitcast.8), calls=%async_computation | async-start | bytes 8388608 | tf_op jit(solution)/shard_map/all_to_all | solution.py:257
  122.5 3.8 %collective-permute-start = (f32[256,512]{1,0:T(8,128)}, f32[256,512]{1,0:T(8,128)S(1)}, u32[]{:S(2)}, u32[]{:S(2)}) collective-permute-start(f32[256,512]{1,0:T(8,128)} %get-tuple-element.5), channel_id=1, source_target_pairs={{0,4},{4,0},{1,5},{5,1},{2,6},{6,2},{3,7},{7,3},{8,12},{12,8},{9,1... | collective-permute-start | bytes 1572872 | tf_op jit(solution)/shard_map/ppermute | solution.py:274
  169.6 5.4 %collective-permute-start.1 = (f32[256,512]{1,0:T(8,128)S(1)}, f32[256,512]{1,0:T(8,128)S(1)}, u32[]{:S(2)}, u32[]{:S(2)}) collective-permute-start(f32[256,512]{1,0:T(8,128)S(1)} %bitcast.6), channel_id=1, source_target_pairs={{0,4},{4,0},{1,5},{5,1},{2,6},{6,2},{3,7},{7,3},{8,12},{12,8},{9,1... | collective-permute-start | bytes 1572872 | tf_op jit(solution)/shard_map/ppermute | solution.py:278
  175.0 2.2 copy-start

commit v2 on v1

v2 whole, which is shorter than its diff:
```python
import functools
import numpy as np
import jax
import jax.numpy as jnp
from jax import lax
from jax.sharding import Mesh
from jax.sharding import PartitionSpec as P
from jax.experimental import pallas as pl
from jax.experimental.pallas import tpu as pltpu

F32, BF16 = jnp.float32, jnp.bfloat16
NT = (((1,), (1,)), ((), ()))
TN = (((0,), (0,)), ((), ()))


def cosine64(size):
    freq = np.arange(size)[:, None]
    place = np.arange(size)[None, :]
    weight = np.where(freq == 0, 1.0, 2.0) / size
    return np.sqrt(weight) * np.cos(np.pi * ((2 * place + 1) * freq % (4 * size)) / (2 * size))


def two(table):
    high = table.astype(np.float32).astype(jnp.bfloat16)
    low = (table - high.astype(np.float64)).astype(np.float32).astype(jnp.bfloat16)
    return high, low


def inner_tables():
    table = cosine64(256)
    swapped = table.reshape(32, 2, 4, 256)[:, ::-1].reshape(256, 256)
    return two(np.stack([table, swapped]))


def split(x):
    high = x.astype(BF16)
    return high, (x - high.astype(F32)).astype(BF16)


def dot(a, b, dims=(((1,), (0,)), ((), ()))):
    return lax.dot_general(a, b, dims, preferred_element_type=F32)


def inner_kernel(start, sign_ref, high_ref, low_ref, x_ref, out_ref):
    results = []
    for s in range(2):
        place = 4 * (start + pl.program_id(0)) + 2 * s
        bits = jnp.concatenate([sign_ref[pl.ds(place, 1), :], sign_ref[pl.ds(place + 1, 1), :]], axis=1)
        sign = (1 - 2 * bits).astype(F32).astype(BF16)
        ch, cl = high_ref[s] * sign, low_ref[s] * sign
        xh, xl = split(x_ref[s * 256 : (s + 1) * 256, :])
        results.append((dot(ch, xh) + (dot(cl, xh) + dot(ch, xl))).reshape(32, 8, 512))
    first, second = results
    upper = lax.broadcasted_iota(jnp.int32, first.shape, 1) < 4
    out_ref[:, 0, 0] = jnp.where(upper, first, second)
    out_ref[:, 1, 0] = jnp.where(upper, second, first)


def inner(matrix, sign_bits, start, count):
    high, low = inner_tables()
    whole = pl.BlockSpec((2, 256, 256), lambda b: (0, 0, 0))
    return pl.pallas_call(
        functools.partial(inner_kernel, start),
        grid=(count,),
        in_specs=[
            pl.BlockSpec((matrix.shape[0] // 128, 128), lambda b: (0, 0)),
            whole,
            whole,
            pl.BlockSpec((512, 512), lambda b: (start + b, 0)),
        ],
        out_specs=pl.BlockSpec((32, 2, 1, 8, 512), lambda b: (0, 0, b, 0, 0)),
        out_shape=jax.ShapeDtypeStruct((32, 2, count, 8, 512), F32),
        cost_estimate=pl.CostEstimate(flops=count * 6 * 512 * 256 * 512, bytes_accessed=count * 2**21, transcendentals=0),
        name="inner",
    )(sign_bits.reshape(-1, 128), jnp.asarray(high), jnp.asarray(low), matrix)


def parity_kernel(first_ref, samples_ref, out_ref):
    batches, half = samples_ref.shape[0], samples_ref.shape[1]
    first = first_ref[0]
    step = 2048
    for b in range(batches):
        total = jnp.zeros((8, 128), F32)
        for start in range(0, half, step):
            pos = samples_ref[b : b + 1, start : start + step]
            a = lax.shift_right_logical(pos, 8)
            pair = lax.shift_right_logical(lax.bitwise_and(pos, 255), 1) - first
            odd = lax.bitwise_and(pos, 1)
            rows = lax.broadcasted_iota(jnp.int32, (128, step), 0)
            hot = (rows == a).astype(F32).astype(BF16)
            which = lax.broadcasted_iota(jnp.int32, (8, step), 0)
            mine = jnp.where(which == pair, odd, 0).astype(F32).astype(BF16)
            total = total + dot(mine, hot, NT)
        out_ref[b] = total


def parity(samples, first_pair):
    batches, half = samples.shape
    return pl.pallas_call(
        parity_kernel,
        grid_spec=pltpu.PrefetchScalarGridSpec(
            num_scalar_prefetch=1,
            grid=(1,),
            in_specs=[pl.BlockSpec((batches, half), lambda i, f: (0, 0))],
            out_specs=pl.BlockSpec((batches, 8, 128), lambda i, f: (0, 0, 0)),
        ),
        out_shape=jax.ShapeDtypeStruct((batches, 8, 128), F32),
        cost_estimate=pl.CostEstimate(flops=2 * batches * half * 128 * 8, bytes_accessed=4 * batches * half, transcendentals=0),
        name="parity",
    )(first_pair, samples)


def outer_kernel(scale, steps, par_ref, odd_ref, high_ref, low_ref, z_ref, prev_ref, *refs):
    step = pl.program_id(0)
    acc_ref, wide_ref = refs[-2:]

    @pl.when(step == 0)
    def _():
        acc_ref[...] = jnp.zeros((512, 512), F32) if prev_ref is None else prev_ref[...]
        place = lax.broadcasted_iota(jnp.int32, (128, 512), 0)
        col = lax.broadcasted_iota(jnp.int32, (128, 512), 1)
        source = 2 * lax.shift_right_logical(col, 3) + lax.bitwise_xor(
            lax.bitwise_and(lax.shift_right_logical(col, 2), 1), par_ref[0]
        )
        pick = jnp.where(place == source, 1.0, 0.0).astype(BF16)
        wide_ref[0] = dot(high_ref[...], pick).astype(BF16)
        wide_ref[1] = dot(low_ref[...], pick).astype(BF16)

    z = z_ref[:, 0].reshape(512, 512)
    zh, zl = split(z)
    row = lax.broadcasted_iota(jnp.int32, (256, 512), 0)
    col = lax.broadcasted_iota(jnp.int32, (256, 512), 1)
    choice = 2 * lax.shift_right_logical(row, 7) + odd_ref[0].astype(jnp.int32)
    keep = jnp.where(lax.bitwise_and(col, 3) == choice, 1.0, 0.0).astype(BF16)
    wh = jnp.concatenate([wide_ref[0]] * 2, axis=0) * keep
    wl = jnp.concatenate([wide_ref[1]] * 2, axis=0) * keep
    rows = dot(wh, zh) + (dot(wl, zh) + dot(wh, zl))
    rh, rl = split(rows)
    acc_ref[...] += dot(rh, rh, TN) + (dot(rh, rl, TN) + dot(rl, rh, TN))

    @pl.when(step == steps - 1)
    def _():
        if scale is None:
            refs[0][...] = acc_ref[...]
        else:
            mine = pl.multiple_of(256 * par_ref[0], 256)
            refs[0][...] = acc_ref[pl.ds(mine, 256), :] * scale
            refs[1][...] = acc_ref[pl.ds(256 - mine, 256), :] * scale


def outer(mixed, odd, start, par, prev, scale):
    count = mixed.shape[1]
    high, low = two(cosine64(128))
    table = pl.BlockSpec((128, 128), lambda b, p: (0, 0))
    whole = pl.BlockSpec((512, 512), lambda b, p: (0, 0))
    half = pl.BlockSpec((256, 512), lambda b, p: (0, 0))
    body = functools.partial(outer_kernel, scale, count)
    if prev is None:
        kernel = lambda p, o, h, l, z, *refs: body(p, o, h, l, z, None, *refs)
    else:
        kernel = body
    return pl.pallas_call(
        kernel,
        grid_spec=pltpu.PrefetchScalarGridSpec(
            num_scalar_prefetch=1,
            grid=(count,),
            in_specs=[
                pl.BlockSpec((1, 256, 1), lambda b, p: (start + b, 0, 0)),
                table,
                table,
                pl.BlockSpec((64, 1, 8, 512), lambda b, p: (0, b, 0, 0)),
            ]
            + ([] if prev is None else [whole]),
            out_specs=whole if scale is None else [half, half],
            scratch_shapes=[pltpu.VMEM((512, 512), F32), pltpu.VMEM((2, 128, 512), BF16)],
        ),
        out_shape=jax.ShapeDtypeStruct((512, 512), F32)
        if scale is None
        else [jax.ShapeDtypeStruct((256, 512), F32)] * 2,
        cost_estimate=pl.CostEstimate(flops=count * 12 * 256 * 512 * 512, bytes_accessed=count * 2**20, transcendentals=0),
        name="outer",
    )(par, odd, jnp.asarray(high), jnp.asarray(low), mixed, *([] if prev is None else [prev]))


def hdot(a, b, dims=(((1,), (0,)), ((), ()))):
    return lax.dot_general(a, b, dims, precision=lax.Precision.HIGHEST, preferred_element_type=F32)


def factor(block):
    size = block.shape[0]
    lane = lax.broadcasted_iota(jnp.int32, (8, size), 1)
    sub = lax.broadcasted_iota(jnp.int32, (8, size), 0)
    count = size // 8
    rows = [block[8 * i : 8 * i + 8] for i in range(count)]
    pivots = []

    def along(x, c):
        return jnp.broadcast_to(x[:, c : c + 1], (8, size))

    def down(x, j):
        return jnp.broadcast_to(x[j : j + 1, :], (8, size))

    for r in range(count):
        first = 8 * r
        inside = (lane >= first) & (lane < first + 8)
        below = range(r + 1, count)
        cols = {i: [along(rows[i], first + k) for k in range(8)] for i in range(r, count)}
        own = jnp.where(inside, jnp.where(lane - first == sub, 1.0, 0.0), rows[r])
        rest = {i: jnp.where(inside, 0.0, rows[i]) for i in below}
        for j in range(8):
            inverse = 1.0 / down(cols[r][j], j)
            heads = {k: down(cols[r][k], j) for k in range(j + 1, 8)}
            line = down(own, j)
            for i in range(r, count):
                factor = cols[i][j] * inverse
                if i == r:
                    if j == 7:
                        continue
                    factor = jnp.where(sub > j, factor, 0.0)
                for k in range(j + 1, 8):
                    cols[i][k] = cols[i][k] - factor * heads[k]
                if i == r:
                    own = own - factor * line
                else:
                    rest[i] = rest[i] - factor * line
        pivot = cols[r][0]
        for k in range(8):
            own = jnp.where((lane == first + k) & (sub <= k), cols[r][k], own)
            if k > 0:
                pivot = jnp.where(sub == k, cols[r][k], pivot)
        rows[r] = own
        pivots.append(pivot)
        for i in below:
            rows[i] = rest[i]
    return jnp.concatenate(rows, axis=0), jnp.concatenate(pivots, axis=0)


def solve_kernel(par_ref, own_ref, other_ref, x_hbm, r_ref, out_hbm, g_ref, inv_ref, x_ref, xh_ref, xl_ref, out_ref, in_sem, out_sem):
    n, nb = 512, 128
    count = n // nb
    fetch = pltpu.make_async_copy(x_hbm, x_ref, in_sem)
    fetch.start()
    mine = pl.multiple_of(256 * par_ref[0], 256)
    g_ref[pl.ds(mine, 256), :] = own_ref[...]
    g_ref[pl.ds(256 - mine, 256), :] = other_ref[...]
    inv_ref[...] = jnp.zeros((n, n), F32)
    r_ref[...] = jnp.zeros((n, n), F32)
    row = lax.broadcasted_iota(jnp.int32, (nb, nb), 0)
    col = lax.broadcasted_iota(jnp.int32, (nb, nb), 1)
    stores = []
    for k in range(count):
        lo, hi = k * nb, (k + 1) * nb
        m, pivots = factor(g_ref[lo:hi, lo:hi])
        root = lax.rsqrt(pivots)
        root = root * (1.5 - 0.5 * pivots * root * root)
        upper = jnp.where(col >= row, m, 0.0) * root
        linv = jnp.where(col < row, m, jnp.where(col == row, 1.0, 0.0)) * root
        r_ref[lo:hi, lo:hi] = upper
        panels = {}
        for j in range(k + 1, count):
            a, b = j * nb, (j + 1) * nb
            panels[j] = hdot(linv, g_ref[lo:hi, a:b])
            r_ref[lo:hi, a:b] = panels[j]
            for i in range(k + 1, j + 1):
                c, d = i * nb, (i + 1) * nb
                g_ref[c:d, a:b] -= hdot(panels[i], panels[j], TN)
        rinv = linv.T
        inv_ref[lo:hi, lo:hi] = rinv
        if k > 0:
            t = hdot(inv_ref[:lo, :lo], r_ref[:lo, lo:hi])
            inv_ref[:lo, lo:hi] = -hdot(t, rinv)
        if k == 0:
            fetch.wait()
            xh, xl = split(x_ref[...])
            xh_ref[...] = xh
            xl_ref[...] = xl
        ih, il = split(inv_ref[:hi, lo:hi])
        a, b = xh_ref[:, :hi], xl_ref[:, :hi]
        out_ref[k] = dot(a, ih) + (dot(b, ih) + dot(a, il))
        store = pltpu.make_async_copy(out_ref.at[k], out_hbm.at[:, lo:hi], out_sem.at[k])
        store.start()
        stores.append(store)
    for store in stores:
        store.wait()


def solve(par, own, other, matrix):
    rows, n = matrix.shape
    vmem = pl.BlockSpec(memory_space=pltpu.VMEM)
    smem = pl.BlockSpec(memory_space=pltpu.SMEM)
    hbm = pl.BlockSpec(memory_space=pltpu.HBM)
    return pl.pallas_call(
        solve_kernel,
        in_specs=[smem, vmem, vmem, hbm],
        out_specs=(vmem, hbm),
        out_shape=(jax.ShapeDtypeStruct((n, n), F32), jax.ShapeDtypeStruct((rows, n), F32)),
        scratch_shapes=[
            pltpu.VMEM((n, n), F32),
            pltpu.VMEM((n, n), F32),
            pltpu.VMEM((rows, n), F32),
            pltpu.VMEM((rows, n), BF16),
            pltpu.VMEM((rows, n), BF16),
            pltpu.VMEM((n // 128, rows, 128), F32),
            pltpu.SemaphoreType.DMA,
            pltpu.SemaphoreType.DMA((n // 128,)),
        ],
        compiler_params=pltpu.CompilerParams(vmem_limit_bytes=61 * 2**20),
        name="solve",
    )(par, own, other, matrix)


def exchange(x, axes):
    return lax.all_to_all(x, axes, split_axis=0, concat_axis=0, tiled=True)


def spread(x, copies, axes):
    return exchange(jnp.broadcast_to(x[None], (copies,) + x.shape), axes)


def local(matrix, sign_bits, samples):
    batches, half = samples.shape
    core = lax.axis_index("core").astype(jnp.int32)
    device = lax.axis_index(("z", "y", "core")).astype(jnp.int32)
    par = core.reshape(1)
    mixed = []
    start = 0
    for count in (batches,):
        sent = inner(matrix, sign_bits, start, count).reshape(64, count, 8, 512)
        mixed.append(exchange(sent, ("z", "y", "core")))
        start += count
    odd = parity(samples, (2 * device).reshape(1))[:, :2].reshape(batches, 256, 1)
    start, total = 0, None
    for i, count in enumerate((batches,)):
        last = i == len(mixed) - 1
        total = outer(mixed[i], odd, start, par, total, 1.0 / (4 * batches * half) if last else None)
        start += count
    keep, send = total
    swap = [(0, 1), (1, 0)]
    part = keep + lax.ppermute(send, "core", swap)
    part = exchange(part.reshape(16, 16, 512), ("y", "x")).sum(0)
    part = spread(part, 8, "z").sum(0)
    own = spread(part, 16, ("y", "x")).reshape(256, 512)
    other = lax.ppermute(own, "core", swap)
    return solve(par, own, other, matrix)


def solution(mesh):
    parts = Mesh(mesh.devices.reshape(8, 4, 2, 4), ("z", "y", "core", "x"))
    every = ("z", "y", "core", "x")
    return jax.shard_map(
        local,
        mesh=parts,
        in_specs=(P(every, None), P(every), P("x", None)),
        out_specs=(P(), P(every, None)),
        check_vma=False,
    )
```

time: 229 us -> 204 us (0.89)
  Pallas kernels: 71 us -> 47.4 us
    pallas_call x3, Pallas kernels: 65 us -> 41.4 us  [the longest x1 27.7 us: solve(): pl.pallas_call(solve_kernel, in_specs=[smem, vmem, vmem, hbm], out_specs=...]
where the time goes in v2:
time: 204 us
  waiting for transfers between devices  90.1 us (44%)
  Pallas kernels  47.4 us (23%)
  blocking collectives  42 us (21%)
  starting transfers between devices  19.3 us (9%)
  local copies, waits for them, and re-layouts  2.72 us (1%)
    all_to_all x1, waiting for transfers between devices, exchange(): return lax.all_to_all(x, axes, split_axis=0, concat_axis=0, tiled=True)  86.9 us
    all_to_all x3, blocking collectives, exchange(): return lax.all_to_all(x, axes, split_axis=0, concat_axis=0, tiled=True)  42 us
    pallas_call x1, Pallas kernels, solve(): pl.pallas_call(solve_kernel, in_specs=[smem, vmem, vmem, hbm], out_specs=...  27.7 us
    all_to_all x1, starting transfers between devices, exchange(): return lax.all_to_all(x, axes, split_axis=0, concat_axis=0, tiled=True)  13.3 us
    pallas_call x1, Pallas kernels, outer(): pl.pallas_call(kernel, grid_spec=pltpu.PrefetchScalarGridSpec(num_scalar_...  7.68 us
    pallas_call x1, Pallas kernels, parity(): pl.pallas_call(parity_kernel, grid_spec=pltpu.PrefetchScalarGridSpec(num_...  5.99 us
    pallas_call x1, Pallas kernels, inner(): pl.pallas_call(functools.partial(inner_kernel, start), grid=(count,), in_...  5.99 us
  transfers between devices with their start and end apart: 3, of which 3 were waited for; matrix products, arithmetic and copies ran while one was open for 1% of the time, Pallas kernels for 3%

profile of v2, /device:TPU:1, one launch (start us, length us, event | category | flops | bytes accessed | tf_op | source)
XLA Modules:
  0.0 203.5 jit_solution(10683508268286832133)
XLA Ops:
  0.6 6.0 %inner.1 = f32[32,2,4,8,512]{4,3,2,1,0:T(8,128)} custom-call(s32[16,128]{1,0:T(8,128)} %bitcast.10, bf16[2,256,256]{2,1,0:T(8,128)(2,1)} %constant.29.clone.high_ref, bf16[2,256,256]{2,1,0:T(8,128)(2,1)} %constant.30.clone.low_ref, f32[2048,512]{1,0:T(8,128)} %x_hbm.1), custom_call_target="tpu_custom_call" | custom-call | flops 1610612736 | bytes 8388608 | tf_op jit(solution)/shard_map/inner/pallas_call | solution.py:62
  6.6 13.3 %all-to-all-start = ((f32[64,4,8,512]{3,2,1,0:T(8,128)}), f32[64,4,8,512]{3,2,1,0:T(8,128)}, u32[]{:S(2)}, u32[]{:S(2)}) async-start(f32[64,4,8,512]{3,2,1,0:T(8,128)} %bitcast.6), calls=%async_computation | async-start | bytes 8388608 | tf_op jit(solution)/shard_map/all_to_all | solution.py:313
  19.9 6.0 %parity.1 = f32[4,8,128]{2,1,0:T(8,128)} custom-call(s32[1]{0:T(128)} %bitcast.1.first_ref, s32[4,16384]{1,0:T(4,128)} %samples_ref.1), custom_call_target="tpu_custom_call" | custom-call | flops 134217728 | bytes 262144 | tf_op jit(solution)/shard_map/parity/pallas_call | solution.py:99
  25.9 0.7 slice.4
  26.6 1.1 reshape.34.o
  27.8 86.9 %all-to-all-done.z = f32[64,4,8,512]{3,2,1,0:T(8,128)} async-done(((f32[64,4,8,512]{3,2,1,0:T(8,128)}), f32[64,4,8,512]{3,2,1,0:T(8,128)}, u32[]{:S(2)}, u32[]{:S(2)}) %all-to-all-start) | async-done | bytes 4194336 | tf_op jit(solution)/shard_map/all_to_all | solution.py:313
  114.6 7.7 %outer.1 = (f32[256,512]{1,0:T(8,128)}, f32[256,512]{1,0:T(8,128)}) custom-call(s32[1]{0:T(128)} %bitcast.p.par_ref, f32[4,256,1]{2,1,0:T(8,128)} %reshape.34.o, bf16[128,128]{1,0:T(8,128)(2,1)} %constant.31.clone.h, bf16[128,128]{1,0:T(8,128)(2,1)} %constant.32.clone.l, f32[64,4,8,512]{3,2,1,0:T(8,128)} %all-to-all-done.z), custom_call_target="tpu_custom_call" | custom-call | flops 3221225472 | bytes 4194304 | tf_op jit(solution)/shard_map/outer/pallas_call | solution.py:162
  122.3 2.1 %collective-permute-start = (f32[256,512]{1,0:T(8,128)}, f32[256,512]{1,0:T(8,128)S(1)}, u32[]{:S(2)}, u32[]{:S(2)}) collective-permute-start(f32[256,512]{1,0:T(8,128)} %get-tuple-element.5), channel_id=1, source_target_pairs={{0,4},{4,0},{1,5},{5,1},{2,6},{6,2},{3,7},{7,3},{8,12},{12,8},{9,1... | collective-permute-start | bytes 1572872 | tf_op jit(solution)/shard_map/ppermute | solution.py:339
  124.4 1.7 collective-permute-done
  126.1 1.1 add.11
  127.2 17.0 %all_to_all.20 = f32[16,16,512]{2,1,0:T(8,128)S(1)} all-to-all(f32[16,16,512]{2,1,0:T(8,128)S(1)} %bitcast.7), channel_id=1, replica_groups=mesh['z'=8,'y'=4,'core'=2,'x'=4] {'y','x'}, dimensions={0} | all-to-all | bytes 1048576 | tf_op jit(solution)/shard_map/all_to_all | solution.py:313
  144.3 12.1 %all_to_all.21 = f32[8,16,512]{2,1,0:T(8,128)S(1)} all-to-all(f32[8,16,512]{2,1,0:T(8,128)S(1)} %broadcast_in_dim.4), channel_id=1, replica_groups=mesh['z'=8,'y'=4,'core'=2,'x'=4] {'z'}, dimensions={0} | all-to-all | bytes 524288 | tf_op jit(solution)/shard_map/all_to_all | solution.py:313
  156.5 0.1 broadcast_in_dim.5
  156.5 12.9 %all_to_all.22 = f32[16,16,512]{2,1,0:T(8,128)S(1)} all-to-all(f32[16,16,512]{2,1,0:T(8,128)S(1)} %broadcast_in_dim.5), channel_id=1, replica_groups=mesh['z'=8,'y'=4,'core'=2,'x'=4] {'y','x'}, dimensions={0} | all-to-all | bytes 1048576 | tf_op jit(solution)/shard_map/all_to_all | solution.py:313
  169.4 0.0 copy-start
  169.4 3.9 %collective-permute-start.1 = (f32[256,512]{1,0:T(8,128)S(1)}, f32[256,512]{1,0:T(8,128)S(1)}, u32[]{:S(2)}, u32[]{:S(2)}) collective-permute-start(f32[256,512]{1,0:T(8,128)S(1)} %bitcast.8), channel_id=1, source_target_pairs={{0,4},{4,0},{1,5},{5,1},{2,6},{6,2},{3,7},{7,3},{8,12},{12,8},{9,1... | collective-permute-start | bytes 1572872 | tf_op jit(solution)/shard_map/ppermute | solution.py:343
  173.3 1.5 collective-permute-done.1.other_ref
  174.8 0.0 copy-done
  174.8 0.0 copy-start.1
  174.8 0.8 copy-done.1
  175.6 27.7 %solve.1 = (f32[512,512]{1,0:T(8,128)}, f32[2048,512]{1,0:T(8,128)}) custom-call(s32[1]{0:T(128)} %bitcast.p.par_ref, f32[256,512]{1,0:T(8,128)} %bitcast.9, f32[256,512]{1,0:T(8,128)} %copy-done.1, f32[2048,512]{1,0:T(8,128)} %x_hbm.1), custom_call_target="tpu_custom_call" | custom-call | tf_op jit(solution)/shard_map/solve/pallas_call | solution.py:292
  (3 shorter events, 0.1 us)
Async XLA Ops:
  6.6 108.0 %all-to-all-start = ((f32[64,4,8,512]{3,2,1,0:T(8,128)}), f32[64,4,8,512]{3,2,1,0:T(8,128)}, u32[]{:S(2)}, u32[]{:S(2)}) async-start(f32[64,4,8,512]{3,2,1,0:T(8,128)} %bitcast.6), calls=%async_computation | async-start | bytes 8388608 | tf_op jit(solution)/shard_map/all_to_all | solution.py:313
  122.3 3.8 %collective-permute-start = (f32[256,512]{1,0:T(8,128)}, f32[256,512]{1,0:T(8,128)S(1)}, u32[]{:S(2)}, u32[]{:S(2)}) collective-permute-start(f32[256,512]{1,0:T(8,128)} %get-tuple-element.5), channel_id=1, source_target_pairs={{0,4},{4,0},{1,5},{5,1},{2,6},{6,2},{3,7},{7,3},{8,12},{12,8},{9,1... | collective-permute-start | bytes 1572872 | tf_op jit(solution)/shard_map/ppermute | solution.py:339
  169.4 5.4 %copy-start = (f32[16,16,512]{2,1,0:T(8,128)}, f32[16,16,512]{2,1,0:T(8,128)S(1)}, u32[]{:S(2)}) copy-start(f32[16,16,512]{2,1,0:T(8,128)S(1)} %all_to_all.22) | copy-start | bytes 1572868
  169.4 5.4 %collective-permute-start.1 = (f32[256,512]{1,0:T(8,128)S(1)}, f32[256,512]{1,0:T(8,128)S(1)}, u32[]{:S(2)}, u32[]{:S(2)}) collective-permute-start(f32[256,512]{1,0:T(8,128)S(1)} %bitcast.8), channel_id=1, source_target_pairs={{0,4},{4,0},{1,5},{5,1},{2,6},{6,2},{3,7},{7,3},{8,12},{12,8},{9,1... | collective-permute-start | bytes 1572872 | tf_op jit(solution)/shard_map/ppermute | solution.py:343
  174.8 0.8 copy-start.1

commit v3 on v2

--- a/solution.py
+++ b/solution.py
@@ -186,12 +186,29 @@
     return lax.dot_general(a, b, dims, precision=lax.Precision.HIGHEST, preferred_element_type=F32)
 
 
+PANEL, GROUP = 32, 16
+
+
+def thirds(x):
+    first = x.astype(BF16)
+    rest = x - first.astype(F32)
+    second = rest.astype(BF16)
+    return first, second, (rest - second.astype(F32)).astype(BF16)
+
+
+def sixfold(a, b):
+    ap, bp = thirds(a), thirds(b)
+    order = ((2, 0), (0, 2), (1, 1), (1, 0), (0, 1), (0, 0))
+    return dot(
+        jnp.concatenate([ap[p] for p, _ in order], axis=0), jnp.concatenate([bp[q] for _, q in order], axis=0), TN
+    )
+
+
 def factor(block):
     size = block.shape[0]
     lane = lax.broadcasted_iota(jnp.int32, (8, size), 1)
     sub = lax.broadcasted_iota(jnp.int32, (8, size), 0)
-    count = size // 8
-    rows = [block[8 * i : 8 * i + 8] for i in range(count)]
+    rows = [block[8 * i : 8 * i + 8] for i in range(size // 8)]
     pivots = []
 
     def along(x, c):
@@ -200,42 +217,70 @@
     def down(x, j):
         return jnp.broadcast_to(x[j : j + 1, :], (8, size))
 
-    for r in range(count):
-        first = 8 * r
-        inside = (lane >= first) & (lane < first + 8)
-        below = range(r + 1, count)
-        cols = {i: [along(rows[i], first + k) for k in range(8)] for i in range(r, count)}
-        own = jnp.where(inside, jnp.where(lane - first == sub, 1.0, 0.0), rows[r])
-        rest = {i: jnp.where(inside, 0.0, rows[i]) for i in below}
-        for j in range(8):
-            inverse = 1.0 / down(cols[r][j], j)
-            heads = {k: down(cols[r][k], j) for k in range(j + 1, 8)}
-            line = down(own, j)
-            for i in range(r, count):
-                factor = cols[i][j] * inverse
-                if i == r:
-                    if j == 7:
+    def within(start, stop):
+        return (lane >= start) & (lane < stop)
+
+    for base in range(0, size, PANEL):
+        end = base + PANEL
+        for first in range(base, end, GROUP):
+            mine = range(first // 8, (first + GROUP) // 8)
+            below = range((first + GROUP) // 8, end // 8)
+            inside = within(first, first + GROUP)
+            cols = {}
+            for k in range(GROUP):
+                for i in (*mine, *below):
+                    cols[i, k] = along(rows[i], first + k)
+            for i in mine:
+                rows[i] = jnp.where(inside, jnp.where(lane == sub + 8 * i, 1.0, 0.0), rows[i])
+            for i in below:
+                rows[i] = jnp.where(inside, 0.0, rows[i])
+            for j in range(GROUP):
+                at, r = (first + j) // 8, j % 8
+                inverse = 1.0 / down(cols[at, j], r)
+                heads = {k: down(cols[at, k], r) for k in range(j + 1, GROUP)}
+                line = down(rows[at], r)
+                for i in range(at, end // 8):
+                    if i == at and r == 7:
                         continue
-                    factor = jnp.where(sub > j, factor, 0.0)
-                for k in range(j + 1, 8):
-                    cols[i][k] = cols[i][k] - factor * heads[k]
-                if i == r:
-                    own = own - factor * line
-                else:
-                    rest[i] = rest[i] - factor * line
-        pivot = cols[r][0]
-        for k in range(8):
-            own = jnp.where((lane == first + k) & (sub <= k), cols[r][k], own)
-            if k > 0:
-                pivot = jnp.where(sub == k, cols[r][k], pivot)
-        rows[r] = own
-        pivots.append(pivot)
-        for i in below:
-            rows[i] = rest[i]
+                    multiple = cols[i, j] * inverse
+                    if i == at:
+                        multiple = jnp.where(sub > r, multiple, 0.0)
+                    for k in range(j + 1, GROUP):
+                        cols[i, k] = cols[i, k] - multiple * heads[k]
+                    rows[i] = rows[i] - multiple * line
+            for i in mine:
+                pivot = cols[i, 8 * i - first]
+                for k in range(GROUP):
+                    rows[i] = jnp.where((lane == first + k) & (sub + 8 * i <= first + k), cols[i, k], rows[i])
+                    if 0 < first + k - 8 * i < 8:
+                        pivot = jnp.where(sub == first + k - 8 * i, cols[i, k], pivot)
+                pivots.append(pivot)
+        if end < size:
+            mine = range(base // 8, end // 8)
+            inside = within(base, end)
+            left = [jnp.where(lane >= end, rows[i] / pivots[i], 0.0) for i in mine]
+            right = []
+            for i in mine:
+                unit = jnp.where(lane == sub + 8 * i, 1.0, jnp.where(lane > sub + 8 * i, 0.0, rows[i]))
+                right.append(jnp.where(inside, unit, rows[i]))
+            change = sixfold(jnp.concatenate(left, axis=0), jnp.concatenate(right, axis=0))
+            for i in range(end // 8, size // 8):
+                rows[i] = jnp.where(inside, 0.0, rows[i]) - change[8 * i : 8 * i + 8]
     return jnp.concatenate(rows, axis=0), jnp.concatenate(pivots, axis=0)
 
 
-def solve_kernel(par_ref, own_ref, other_ref, x_hbm, r_ref, out_hbm, g_ref, inv_ref, x_ref, xh_ref, xl_ref, out_ref, in_sem, out_sem):
+def product(lhs, blocks):
+    n = blocks[0].shape[1]
+    stack = []
+    for block in blocks:
+        high, low = split(block)
+        stack.append(jnp.concatenate([high, low], axis=1))
+        stack.append(jnp.concatenate([high, jnp.zeros_like(low)], axis=1))
+    both = dot(lhs, jnp.concatenate(stack, axis=0))
+    return both[:, :n] + both[:, n:]
+
+
+def solve_kernel(par_ref, own_ref, other_ref, x_hbm, r_ref, out_hbm, g_ref, inv_ref, x_ref, xs_ref, out_ref, in_sem, out_sem):
     n, nb = 512, 128
     count = n // nb
     fetch = pltpu.make_async_copy(x_hbm, x_ref, in_sem)
@@ -250,6 +295,10 @@
     stores = []
     for k in range(count):
         lo, hi = k * nb, (k + 1) * nb
+        if k > 0:
+            t = hdot(inv_ref[:lo, :lo], r_ref[:lo, lo:hi])
+            base = x_ref[:, lo:hi] - product(xs_ref[:, : 2 * lo], [t[i : i + nb] for i in range(0, lo, nb)])
+            lhs = jnp.concatenate(split(base), axis=1)
         m, pivots = factor(g_ref[lo:hi, lo:hi])
         root = lax.rsqrt(pivots)
         root = root * (1.5 - 0.5 * pivots * root * root)
@@ -265,18 +314,16 @@
                 c, d = i * nb, (i + 1) * nb
                 g_ref[c:d, a:b] -= hdot(panels[i], panels[j], TN)
         rinv = linv.T
-        inv_ref[lo:hi, lo:hi] = rinv
-        if k > 0:
-            t = hdot(inv_ref[:lo, :lo], r_ref[:lo, lo:hi])
-            inv_ref[:lo, lo:hi] = -hdot(t, rinv)
+        if k + 1 < count:
+            inv_ref[lo:hi, lo:hi] = rinv
+            if k > 0:
+                inv_ref[:lo, lo:hi] = -hdot(t, rinv)
         if k == 0:
             fetch.wait()
-            xh, xl = split(x_ref[...])
-            xh_ref[...] = xh
-            xl_ref[...] = xl
-        ih, il = split(inv_ref[:hi, lo:hi])
-        a, b = xh_ref[:, :hi], xl_ref[:, :hi]
-        out_ref[k] = dot(a, ih) + (dot(b, ih) + dot(a, il))
+            for i in range(count):
+                xs_ref[:, 2 * i * nb : 2 * (i + 1) * nb] = jnp.concatenate(split(x_ref[:, i * nb : (i + 1) * nb]), axis=1)
+            lhs = xs_ref[:, : 2 * nb]
+        out_ref[k] = product(lhs, [rinv])
         store = pltpu.make_async_copy(out_ref.at[k], out_hbm.at[:, lo:hi], out_sem.at[k])
         store.start()
         stores.append(store)
@@ -298,8 +345,7 @@
             pltpu.VMEM((n, n), F32),
             pltpu.VMEM((n, n), F32),
             pltpu.VMEM((rows, n), F32),
-            pltpu.VMEM((rows, n), BF16),
-            pltpu.VMEM((rows, n), BF16),
+            pltpu.VMEM((rows, 2 * n), BF16),
             pltpu.VMEM((n // 128, rows, 128), F32),
             pltpu.SemaphoreType.DMA,
             pltpu.SemaphoreType.DMA((n // 128,)),

time: 204 us -> 196 us (0.961)
  Pallas kernels: 47.4 us -> 39.3 us
    pallas_call x1, Pallas kernels: 27.7 us -> 19.7 us  [solve(): pl.pallas_call(solve_kernel, in_specs=[smem, vmem, vmem, hbm], out_specs=...]
where the time goes in v3:
time: 196 us; the launch traced here: 195 us
  waiting for transfers between devices  90.1 us (46%)
  blocking collectives  42 us (21%)
  Pallas kernels  39.3 us (20%)
  starting transfers between devices  19.3 us (10%)
  local copies, waits for them, and re-layouts  2.72 us (1%)
    all_to_all x1, waiting for transfers between devices, exchange(): return lax.all_to_all(x, axes, split_axis=0, concat_axis=0, tiled=True)  86.9 us
    all_to_all x3, blocking collectives, exchange(): return lax.all_to_all(x, axes, split_axis=0, concat_axis=0, tiled=True)  42 us
    pallas_call x1, Pallas kernels, solve(): pl.pallas_call(solve_kernel, in_specs=[smem, vmem, vmem, hbm], out_specs=...  19.7 us
    all_to_all x1, starting transfers between devices, exchange(): return lax.all_to_all(x, axes, split_axis=0, concat_axis=0, tiled=True)  13.3 us
    pallas_call x1, Pallas kernels, outer(): pl.pallas_call(kernel, grid_spec=pltpu.PrefetchScalarGridSpec(num_scalar_...  7.68 us
    pallas_call x1, Pallas kernels, parity(): pl.pallas_call(parity_kernel, grid_spec=pltpu.PrefetchScalarGridSpec(num_...  5.99 us
    pallas_call x1, Pallas kernels, inner(): pl.pallas_call(functools.partial(inner_kernel, start), grid=(count,), in_...  5.99 us
  transfers between devices with their start and end apart: 3, of which 3 were waited for; matrix products, arithmetic and copies ran while one was open for 1% of the time, Pallas kernels for 3%

profile of v3, /device:TPU:1, one launch (start us, length us, event | category | flops | bytes accessed | tf_op | source)
XLA Modules:
  0.0 195.5 jit_solution(12390628610332396873)
XLA Ops:
  0.6 6.0 %inner.1 = f32[32,2,4,8,512]{4,3,2,1,0:T(8,128)} custom-call(s32[16,128]{1,0:T(8,128)} %bitcast.10, bf16[2,256,256]{2,1,0:T(8,128)(2,1)} %constant.29.clone.high_ref, bf16[2,256,256]{2,1,0:T(8,128)(2,1)} %constant.30.clone.low_ref, f32[2048,512]{1,0:T(8,128)} %x_hbm.1), custom_call_target="tpu_custom_call" | custom-call | flops 1610612736 | bytes 8388608 | tf_op jit(solution)/shard_map/inner/pallas_call | solution.py:62
  6.6 13.3 %all-to-all-start = ((f32[64,4,8,512]{3,2,1,0:T(8,128)}), f32[64,4,8,512]{3,2,1,0:T(8,128)}, u32[]{:S(2)}, u32[]{:S(2)}) async-start(f32[64,4,8,512]{3,2,1,0:T(8,128)} %bitcast.6), calls=%async_computation | async-start | bytes 8388608 | tf_op jit(solution)/shard_map/all_to_all | solution.py:359
  19.9 6.0 %parity.1 = f32[4,8,128]{2,1,0:T(8,128)} custom-call(s32[1]{0:T(128)} %bitcast.1.first_ref, s32[4,16384]{1,0:T(4,128)} %samples_ref.1), custom_call_target="tpu_custom_call" | custom-call | flops 134217728 | bytes 262144 | tf_op jit(solution)/shard_map/parity/pallas_call | solution.py:99
  25.9 0.7 slice.4
  26.6 1.1 reshape.34.o
  27.8 86.9 %all-to-all-done.z = f32[64,4,8,512]{3,2,1,0:T(8,128)} async-done(((f32[64,4,8,512]{3,2,1,0:T(8,128)}), f32[64,4,8,512]{3,2,1,0:T(8,128)}, u32[]{:S(2)}, u32[]{:S(2)}) %all-to-all-start) | async-done | bytes 4194336 | tf_op jit(solution)/shard_map/all_to_all | solution.py:359
  114.6 7.7 %outer.1 = (f32[256,512]{1,0:T(8,128)}, f32[256,512]{1,0:T(8,128)}) custom-call(s32[1]{0:T(128)} %bitcast.p.par_ref, f32[4,256,1]{2,1,0:T(8,128)} %reshape.34.o, bf16[128,128]{1,0:T(8,128)(2,1)} %constant.31.clone.h, bf16[128,128]{1,0:T(8,128)(2,1)} %constant.32.clone.l, f32[64,4,8,512]{3,2,1,0:T(8,128)} %all-to-all-done.z), custom_call_target="tpu_custom_call" | custom-call | flops 3221225472 | bytes 4194304 | tf_op jit(solution)/shard_map/outer/pallas_call | solution.py:162
  122.3 2.1 %collective-permute-start = (f32[256,512]{1,0:T(8,128)}, f32[256,512]{1,0:T(8,128)S(1)}, u32[]{:S(2)}, u32[]{:S(2)}) collective-permute-start(f32[256,512]{1,0:T(8,128)} %get-tuple-element.5), channel_id=1, source_target_pairs={{0,4},{4,0},{1,5},{5,1},{2,6},{6,2},{3,7},{7,3},{8,12},{12,8},{9,1... | collective-permute-start | bytes 1572872 | tf_op jit(solution)/shard_map/ppermute | solution.py:385
  124.4 1.7 collective-permute-done
  126.1 1.1 add.11
  127.2 17.0 %all_to_all.20 = f32[16,16,512]{2,1,0:T(8,128)S(1)} all-to-all(f32[16,16,512]{2,1,0:T(8,128)S(1)} %bitcast.7), channel_id=1, replica_groups=mesh['z'=8,'y'=4,'core'=2,'x'=4] {'y','x'}, dimensions={0} | all-to-all | bytes 1048576 | tf_op jit(solution)/shard_map/all_to_all | solution.py:359
  144.3 12.1 %all_to_all.21 = f32[8,16,512]{2,1,0:T(8,128)S(1)} all-to-all(f32[8,16,512]{2,1,0:T(8,128)S(1)} %broadcast_in_dim.4), channel_id=1, replica_groups=mesh['z'=8,'y'=4,'core'=2,'x'=4] {'z'}, dimensions={0} | all-to-all | bytes 524288 | tf_op jit(solution)/shard_map/all_to_all | solution.py:359
  156.5 0.1 broadcast_in_dim.5
  156.5 12.9 %all_to_all.22 = f32[16,16,512]{2,1,0:T(8,128)S(1)} all-to-all(f32[16,16,512]{2,1,0:T(8,128)S(1)} %broadcast_in_dim.5), channel_id=1, replica_groups=mesh['z'=8,'y'=4,'core'=2,'x'=4] {'y','x'}, dimensions={0} | all-to-all | bytes 1048576 | tf_op jit(solution)/shard_map/all_to_all | solution.py:359
  169.4 0.0 copy-start
  169.4 3.9 %collective-permute-start.1 = (f32[256,512]{1,0:T(8,128)S(1)}, f32[256,512]{1,0:T(8,128)S(1)}, u32[]{:S(2)}, u32[]{:S(2)}) collective-permute-start(f32[256,512]{1,0:T(8,128)S(1)} %bitcast.8), channel_id=1, source_target_pairs={{0,4},{4,0},{1,5},{5,1},{2,6},{6,2},{3,7},{7,3},{8,12},{12,8},{9,1... | collective-permute-start | bytes 1572872 | tf_op jit(solution)/shard_map/ppermute | solution.py:389
  173.3 1.5 collective-permute-done.1.other_ref
  174.8 0.0 copy-done
  174.8 0.0 copy-start.1
  174.8 0.8 copy-done.1
  175.6 19.7 %solve.1 = (f32[512,512]{1,0:T(8,128)}, f32[2048,512]{1,0:T(8,128)}) custom-call(s32[1]{0:T(128)} %bitcast.p.par_ref, f32[256,512]{1,0:T(8,128)} %bitcast.9, f32[256,512]{1,0:T(8,128)} %copy-done.1, f32[2048,512]{1,0:T(8,128)} %x_hbm.1), custom_call_target="tpu_custom_call" | custom-call | tf_op jit(solution)/shard_map/solve/pallas_call | solution.py:339
  (3 shorter events, 0.1 us)
Async XLA Ops:
  6.6 108.0 %all-to-all-start = ((f32[64,4,8,512]{3,2,1,0:T(8,128)}), f32[64,4,8,512]{3,2,1,0:T(8,128)}, u32[]{:S(2)}, u32[]{:S(2)}) async-start(f32[64,4,8,512]{3,2,1,0:T(8,128)} %bitcast.6), calls=%async_computation | async-start | bytes 8388608 | tf_op jit(solution)/shard_map/all_to_all | solution.py:359
  122.3 3.8 %collective-permute-start = (f32[256,512]{1,0:T(8,128)}, f32[256,512]{1,0:T(8,128)S(1)}, u32[]{:S(2)}, u32[]{:S(2)}) collective-permute-start(f32[256,512]{1,0:T(8,128)} %get-tuple-element.5), channel_id=1, source_target_pairs={{0,4},{4,0},{1,5},{5,1},{2,6},{6,2},{3,7},{7,3},{8,12},{12,8},{9,1... | collective-permute-start | bytes 1572872 | tf_op jit(solution)/shard_map/ppermute | solution.py:385
  169.4 5.4 %copy-start = (f32[16,16,512]{2,1,0:T(8,128)}, f32[16,16,512]{2,1,0:T(8,128)S(1)}, u32[]{:S(2)}) copy-start(f32[16,16,512]{2,1,0:T(8,128)S(1)} %all_to_all.22) | copy-start | bytes 1572868
  169.4 5.4 %collective-permute-start.1 = (f32[256,512]{1,0:T(8,128)S(1)}, f32[256,512]{1,0:T(8,128)S(1)}, u32[]{:S(2)}, u32[]{:S(2)}) collective-permute-start(f32[256,512]{1,0:T(8,128)S(1)} %bitcast.8), channel_id=1, source_target_pairs={{0,4},{4,0},{1,5},{5,1},{2,6},{6,2},{3,7},{7,3},{8,12},{12,8},{9,1... | collective-permute-start | bytes 1572872 | tf_op jit(solution)/shard_map/ppermute | solution.py:389
  174.8 0.8 copy-start.1

commit v4 on v3

--- a/solution.py
+++ b/solution.py
@@ -9,6 +9,7 @@
 from jax.experimental.pallas import tpu as pltpu
 
 F32, BF16 = jnp.float32, jnp.bfloat16
+INNER_STEP, OUTER_STEP = 2, 2
 NT = (((1,), (1,)), ((), ()))
 TN = (((0,), (0,)), ((), ()))
 
@@ -41,34 +42,37 @@
     return lax.dot_general(a, b, dims, preferred_element_type=F32)
 
 
-def inner_kernel(start, sign_ref, high_ref, low_ref, x_ref, out_ref):
-    results = []
-    for s in range(2):
-        place = 4 * (start + pl.program_id(0)) + 2 * s
-        bits = jnp.concatenate([sign_ref[pl.ds(place, 1), :], sign_ref[pl.ds(place + 1, 1), :]], axis=1)
-        sign = (1 - 2 * bits).astype(F32).astype(BF16)
-        ch, cl = high_ref[s] * sign, low_ref[s] * sign
-        xh, xl = split(x_ref[s * 256 : (s + 1) * 256, :])
-        results.append((dot(ch, xh) + (dot(cl, xh) + dot(ch, xl))).reshape(32, 8, 512))
-    first, second = results
-    upper = lax.broadcasted_iota(jnp.int32, first.shape, 1) < 4
-    out_ref[:, 0, 0] = jnp.where(upper, first, second)
-    out_ref[:, 1, 0] = jnp.where(upper, second, first)
-
-
-def inner(matrix, sign_bits, start, count):
+def inner_kernel(sign_ref, high_ref, low_ref, x_ref, out_ref):
+    per = out_ref.shape[2]
+    for u in range(per):
+        results = []
+        for s in range(2):
+            place = 4 * (per * pl.program_id(0) + u) + 2 * s
+            bits = jnp.concatenate([sign_ref[pl.ds(place, 1), :], sign_ref[pl.ds(place + 1, 1), :]], axis=1)
+            sign = (1 - 2 * bits).astype(F32).astype(BF16)
+            ch, cl = high_ref[s] * sign, low_ref[s] * sign
+            xh, xl = split(x_ref[512 * u + 256 * s : 512 * u + 256 * (s + 1), :])
+            results.append((dot(ch, xh) + (dot(cl, xh) + dot(ch, xl))).reshape(32, 8, 512))
+        first, second = results
+        upper = lax.broadcasted_iota(jnp.int32, first.shape, 1) < 4
+        out_ref[:, 0, u] = jnp.where(upper, first, second)
+        out_ref[:, 1, u] = jnp.where(upper, second, first)
+
+
+def inner(matrix, sign_bits, per):
+    count = matrix.shape[0] // 512
     high, low = inner_tables()
     whole = pl.BlockSpec((2, 256, 256), lambda b: (0, 0, 0))
     return pl.pallas_call(
-        functools.partial(inner_kernel, start),
-        grid=(count,),
+        inner_kernel,
+        grid=(count // per,),
         in_specs=[
-            pl.BlockSpec((matrix.shape[0] // 128, 128), lambda b: (0, 0)),
+            pl.BlockSpec((4 * count, 128), lambda b: (0, 0)),
             whole,
             whole,
-            pl.BlockSpec((512, 512), lambda b: (start + b, 0)),
+            pl.BlockSpec((512 * per, 512), lambda b: (b, 0)),
         ],
-        out_specs=pl.BlockSpec((32, 2, 1, 8, 512), lambda b: (0, 0, b, 0, 0)),
+        out_specs=pl.BlockSpec((32, 2, per, 8, 512), lambda b: (0, 0, b, 0, 0)),
         out_shape=jax.ShapeDtypeStruct((32, 2, count, 8, 512), F32),
         cost_estimate=pl.CostEstimate(flops=count * 6 * 512 * 256 * 512, bytes_accessed=count * 2**21, transcendentals=0),
         name="inner",
@@ -110,13 +114,12 @@
     )(first_pair, samples)
 
 
-def outer_kernel(scale, steps, par_ref, odd_ref, high_ref, low_ref, z_ref, prev_ref, *refs):
+def outer_kernel(scale, steps, par_ref, odd_ref, high_ref, low_ref, z_ref, keep_ref, send_ref, acc_ref, wide_ref):
     step = pl.program_id(0)
-    acc_ref, wide_ref = refs[-2:]
 
     @pl.when(step == 0)
     def _():
-        acc_ref[...] = jnp.zeros((512, 512), F32) if prev_ref is None else prev_ref[...]
+        acc_ref[...] = jnp.zeros((512, 512), F32)
         place = lax.broadcasted_iota(jnp.int32, (128, 512), 0)
         col = lax.broadcasted_iota(jnp.int32, (128, 512), 1)
         source = 2 * lax.shift_right_logical(col, 3) + lax.bitwise_xor(
@@ -126,60 +129,51 @@
         wide_ref[0] = dot(high_ref[...], pick).astype(BF16)
         wide_ref[1] = dot(low_ref[...], pick).astype(BF16)
 
-    z = z_ref[:, 0].reshape(512, 512)
-    zh, zl = split(z)
-    row = lax.broadcasted_iota(jnp.int32, (256, 512), 0)
-    col = lax.broadcasted_iota(jnp.int32, (256, 512), 1)
-    choice = 2 * lax.shift_right_logical(row, 7) + odd_ref[0].astype(jnp.int32)
-    keep = jnp.where(lax.bitwise_and(col, 3) == choice, 1.0, 0.0).astype(BF16)
-    wh = jnp.concatenate([wide_ref[0]] * 2, axis=0) * keep
-    wl = jnp.concatenate([wide_ref[1]] * 2, axis=0) * keep
-    rows = dot(wh, zh) + (dot(wl, zh) + dot(wh, zl))
-    rh, rl = split(rows)
-    acc_ref[...] += dot(rh, rh, TN) + (dot(rh, rl, TN) + dot(rl, rh, TN))
+    total = None
+    for u in range(z_ref.shape[1]):
+        zh, zl = split(z_ref[:, u].reshape(512, 512))
+        row = lax.broadcasted_iota(jnp.int32, (256, 512), 0)
+        col = lax.broadcasted_iota(jnp.int32, (256, 512), 1)
+        choice = 2 * lax.shift_right_logical(row, 7) + odd_ref[u].astype(jnp.int32)
+        keep = jnp.where(lax.bitwise_and(col, 3) == choice, 1.0, 0.0).astype(BF16)
+        wh = jnp.concatenate([wide_ref[0]] * 2, axis=0) * keep
+        wl = jnp.concatenate([wide_ref[1]] * 2, axis=0) * keep
+        rows = dot(wh, zh) + (dot(wl, zh) + dot(wh, zl))
+        rh, rl = split(rows)
+        part = dot(rh, rh, TN) + (dot(rh, rl, TN) + dot(rl, rh, TN))
+        total = part if total is None else total + part
+    acc_ref[...] += total
 
     @pl.when(step == steps - 1)
     def _():
-        if scale is None:
-            refs[0][...] = acc_ref[...]
-        else:
-            mine = pl.multiple_of(256 * par_ref[0], 256)
-            refs[0][...] = acc_ref[pl.ds(mine, 256), :] * scale
-            refs[1][...] = acc_ref[pl.ds(256 - mine, 256), :] * scale
-
-
-def outer(mixed, odd, start, par, prev, scale):
+        mine = pl.multiple_of(256 * par_ref[0], 256)
+        keep_ref[...] = acc_ref[pl.ds(mine, 256), :] * scale
+        send_ref[...] = acc_ref[pl.ds(256 - mine, 256), :] * scale
+
+
+def outer(mixed, odd, par, scale, per):
     count = mixed.shape[1]
     high, low = two(cosine64(128))
     table = pl.BlockSpec((128, 128), lambda b, p: (0, 0))
-    whole = pl.BlockSpec((512, 512), lambda b, p: (0, 0))
     half = pl.BlockSpec((256, 512), lambda b, p: (0, 0))
-    body = functools.partial(outer_kernel, scale, count)
-    if prev is None:
-        kernel = lambda p, o, h, l, z, *refs: body(p, o, h, l, z, None, *refs)
-    else:
-        kernel = body
     return pl.pallas_call(
-        kernel,
+        functools.partial(outer_kernel, scale, count // per),
         grid_spec=pltpu.PrefetchScalarGridSpec(
             num_scalar_prefetch=1,
-            grid=(count,),
+            grid=(count // per,),
             in_specs=[
-                pl.BlockSpec((1, 256, 1), lambda b, p: (start + b, 0, 0)),
+                pl.BlockSpec((per, 256, 1), lambda b, p: (b, 0, 0)),
                 table,
                 table,
-                pl.BlockSpec((64, 1, 8, 512), lambda b, p: (0, b, 0, 0)),
-            ]
-            + ([] if prev is None else [whole]),
-            out_specs=whole if scale is None else [half, half],
+                pl.BlockSpec((64, per, 8, 512), lambda b, p: (0, b, 0, 0)),
+            ],
+            out_specs=[half, half],
             scratch_shapes=[pltpu.VMEM((512, 512), F32), pltpu.VMEM((2, 128, 512), BF16)],
         ),
-        out_shape=jax.ShapeDtypeStruct((512, 512), F32)
-        if scale is None
-        else [jax.ShapeDtypeStruct((256, 512), F32)] * 2,
+        out_shape=[jax.ShapeDtypeStruct((256, 512), F32)] * 2,
         cost_estimate=pl.CostEstimate(flops=count * 12 * 256 * 512 * 512, bytes_accessed=count * 2**20, transcendentals=0),
         name="outer",
-    )(par, odd, jnp.asarray(high), jnp.asarray(low), mixed, *([] if prev is None else [prev]))
+    )(par, odd, jnp.asarray(high), jnp.asarray(low), mixed)
 
 
 def hdot(a, b, dims=(((1,), (0,)), ((), ()))):
@@ -229,7 +223,7 @@
             cols = {}
             for k in range(GROUP):
                 for i in (*mine, *below):
-                    cols[i, k] = along(rows[i], first + k)
+                    cols[i, k] = along(rows[i], first + k) + 0.0
             for i in mine:
                 rows[i] = jnp.where(inside, jnp.where(lane == sub + 8 * i, 1.0, 0.0), rows[i])
             for i in below:
@@ -368,19 +362,10 @@
     core = lax.axis_index("core").astype(jnp.int32)
     device = lax.axis_index(("z", "y", "core")).astype(jnp.int32)
     par = core.reshape(1)
-    mixed = []
-    start = 0
-    for count in (batches,):
-        sent = inner(matrix, sign_bits, start, count).reshape(64, count, 8, 512)
-        mixed.append(exchange(sent, ("z", "y", "core")))
-        start += count
+    sent = inner(matrix, sign_bits, INNER_STEP).reshape(64, batches, 8, 512)
+    mixed = exchange(sent, ("z", "y", "core"))
     odd = parity(samples, (2 * device).reshape(1))[:, :2].reshape(batches, 256, 1)
-    start, total = 0, None
-    for i, count in enumerate((batches,)):
-        last = i == len(mixed) - 1
-        total = outer(mixed[i], odd, start, par, total, 1.0 / (4 * batches * half) if last else None)
-        start += count
-    keep, send = total
+    keep, send = outer(mixed, odd, par, 1.0 / (4 * batches * half), OUTER_STEP)
     swap = [(0, 1), (1, 0)]
     part = keep + lax.ppermute(send, "core", swap)
     part = exchange(part.reshape(16, 16, 512), ("y", "x")).sum(0)

time: 196 us -> 193 us (0.985)
  Pallas kernels: 39.3 us -> 36.2 us
    pallas_call x1, Pallas kernels: 19.7 us -> 17.6 us  [solve(): pl.pallas_call(solve_kernel, in_specs=[smem, vmem, vmem, hbm], out_specs=...]
where the time goes in v4:
time: 193 us; the launch traced here: 192 us
  waiting for transfers between devices  90.1 us (47%)
  blocking collectives  42 us (22%)
  Pallas kernels  36.2 us (19%)
  starting transfers between devices  19.3 us (10%)
  local copies, waits for them, and re-layouts  2.72 us (1%)
    all_to_all x1, waiting for transfers between devices, exchange(): return lax.all_to_all(x, axes, split_axis=0, concat_axis=0, tiled=True)  86.9 us
    all_to_all x3, blocking collectives, exchange(): return lax.all_to_all(x, axes, split_axis=0, concat_axis=0, tiled=True)  42 us
    pallas_call x1, Pallas kernels, solve(): pl.pallas_call(solve_kernel, in_specs=[smem, vmem, vmem, hbm], out_specs=...  17.6 us
    all_to_all x1, starting transfers between devices, exchange(): return lax.all_to_all(x, axes, split_axis=0, concat_axis=0, tiled=True)  13.3 us
    pallas_call x1, Pallas kernels, outer(): pl.pallas_call(functools.partial(outer_kernel, scale, count // per), grid...  7.5 us
    pallas_call x1, Pallas kernels, parity(): pl.pallas_call(parity_kernel, grid_spec=pltpu.PrefetchScalarGridSpec(num_...  5.99 us
    pallas_call x1, Pallas kernels, inner(): pl.pallas_call(inner_kernel, grid=(count // per,), in_specs=[pl.BlockSpec...  5.09 us
    ppermute x1, starting transfers between devices, local(): other = lax.ppermute(own, 'core', swap)  3.9 us
  transfers between devices with their start and end apart: 3, of which 3 were waited for; matrix products, arithmetic and copies ran while one was open for 1% of the time, Pallas kernels for 3%

profile of v4, /device:TPU:1, one launch (start us, length us, event | category | flops | bytes accessed | tf_op | source)
XLA Modules:
  0.0 192.3 jit_solution(13680098726203602023)
XLA Ops:
  0.6 5.1 %inner.1 = f32[32,2,4,8,512]{4,3,2,1,0:T(8,128)} custom-call(s32[16,128]{1,0:T(8,128)} %bitcast.10, bf16[2,256,256]{2,1,0:T(8,128)(2,1)} %constant.29.clone.high_ref, bf16[2,256,256]{2,1,0:T(8,128)(2,1)} %constant.30.clone.low_ref, f32[2048,512]{1,0:T(8,128)} %x_hbm.1), custom_call_target="tpu_custom_call" | custom-call | flops 1610612736 | bytes 8388608 | tf_op jit(solution)/shard_map/inner/pallas_call | solution.py:66
  5.7 13.3 %all-to-all-start = ((f32[64,4,8,512]{3,2,1,0:T(8,128)}), f32[64,4,8,512]{3,2,1,0:T(8,128)}, u32[]{:S(2)}, u32[]{:S(2)}) async-start(f32[64,4,8,512]{3,2,1,0:T(8,128)} %bitcast.6), calls=%async_computation | async-start | bytes 8388608 | tf_op jit(solution)/shard_map/all_to_all | solution.py:353
  19.1 6.0 %parity.1 = f32[4,8,128]{2,1,0:T(8,128)} custom-call(s32[1]{0:T(128)} %bitcast.1.first_ref, s32[4,16384]{1,0:T(4,128)} %samples_ref.1), custom_call_target="tpu_custom_call" | custom-call | flops 134217728 | bytes 262144 | tf_op jit(solution)/shard_map/parity/pallas_call | solution.py:103
  25.1 0.7 slice.4
  25.8 1.1 reshape.34.odd_ref
  26.9 86.9 %all-to-all-done.z_ref = f32[64,4,8,512]{3,2,1,0:T(8,128)} async-done(((f32[64,4,8,512]{3,2,1,0:T(8,128)}), f32[64,4,8,512]{3,2,1,0:T(8,128)}, u32[]{:S(2)}, u32[]{:S(2)}) %all-to-all-start) | async-done | bytes 4194336 | tf_op jit(solution)/shard_map/all_to_all | solution.py:353
  113.8 7.5 %outer.1 = (f32[256,512]{1,0:T(8,128)}, f32[256,512]{1,0:T(8,128)}) custom-call(s32[1]{0:T(128)} %bitcast.par_ref, f32[4,256,1]{2,1,0:T(8,128)} %reshape.34.odd_ref, bf16[128,128]{1,0:T(8,128)(2,1)} %constant.31.clone.high_ref, bf16[128,128]{1,0:T(8,128)(2,1)} %constant.32.clone.low_ref, f32[64,4,8,512]{3,2,1,0:T(8,128)} %all-to-all-done.z_ref), custom_call_target="tpu_custom_call" | custom-call | flops 3221225472 | bytes 4194304 | tf_op jit(solution)/shard_map/outer/pallas_call | solution.py:159
  121.3 2.1 %collective-permute-start = (f32[256,512]{1,0:T(8,128)}, f32[256,512]{1,0:T(8,128)S(1)}, u32[]{:S(2)}, u32[]{:S(2)}) collective-permute-start(f32[256,512]{1,0:T(8,128)} %get-tuple-element.5), channel_id=1, source_target_pairs={{0,4},{4,0},{1,5},{5,1},{2,6},{6,2},{3,7},{7,3},{8,12},{12,8},{9,1... | collective-permute-start | bytes 1572872 | tf_op jit(solution)/shard_map/ppermute | solution.py:370
  123.3 1.7 collective-permute-done
  125.1 1.1 add.11
  126.2 16.9 %all_to_all.20 = f32[16,16,512]{2,1,0:T(8,128)S(1)} all-to-all(f32[16,16,512]{2,1,0:T(8,128)S(1)} %bitcast.7), channel_id=1, replica_groups=mesh['z'=8,'y'=4,'core'=2,'x'=4] {'y','x'}, dimensions={0} | all-to-all | bytes 1048576 | tf_op jit(solution)/shard_map/all_to_all | solution.py:353
  143.2 12.1 %all_to_all.21 = f32[8,16,512]{2,1,0:T(8,128)S(1)} all-to-all(f32[8,16,512]{2,1,0:T(8,128)S(1)} %broadcast_in_dim.4), channel_id=1, replica_groups=mesh['z'=8,'y'=4,'core'=2,'x'=4] {'z'}, dimensions={0} | all-to-all | bytes 524288 | tf_op jit(solution)/shard_map/all_to_all | solution.py:353
  155.4 0.1 broadcast_in_dim.5
  155.4 12.9 %all_to_all.22 = f32[16,16,512]{2,1,0:T(8,128)S(1)} all-to-all(f32[16,16,512]{2,1,0:T(8,128)S(1)} %broadcast_in_dim.5), channel_id=1, replica_groups=mesh['z'=8,'y'=4,'core'=2,'x'=4] {'y','x'}, dimensions={0} | all-to-all | bytes 1048576 | tf_op jit(solution)/shard_map/all_to_all | solution.py:353
  168.3 0.0 copy-start
  168.3 3.9 %collective-permute-start.1 = (f32[256,512]{1,0:T(8,128)S(1)}, f32[256,512]{1,0:T(8,128)S(1)}, u32[]{:S(2)}, u32[]{:S(2)}) collective-permute-start(f32[256,512]{1,0:T(8,128)S(1)} %bitcast.8), channel_id=1, source_target_pairs={{0,4},{4,0},{1,5},{5,1},{2,6},{6,2},{3,7},{7,3},{8,12},{12,8},{9,1... | collective-permute-start | bytes 1572872 | tf_op jit(solution)/shard_map/ppermute | solution.py:374
  172.2 1.5 collective-permute-done.1.other_ref
  173.8 0.0 copy-done
  173.8 0.0 copy-start.1
  173.8 0.8 copy-done.1
  174.6 17.6 %solve.1 = (f32[512,512]{1,0:T(8,128)}, f32[2048,512]{1,0:T(8,128)}) custom-call(s32[1]{0:T(128)} %bitcast.par_ref, f32[256,512]{1,0:T(8,128)} %bitcast.9, f32[256,512]{1,0:T(8,128)} %copy-done.1, f32[2048,512]{1,0:T(8,128)} %x_hbm.1), custom_call_target="tpu_custom_call" | custom-call | tf_op jit(solution)/shard_map/solve/pallas_call | solution.py:333
  (3 shorter events, 0.1 us)
Async XLA Ops:
  5.7 108.1 %all-to-all-start = ((f32[64,4,8,512]{3,2,1,0:T(8,128)}), f32[64,4,8,512]{3,2,1,0:T(8,128)}, u32[]{:S(2)}, u32[]{:S(2)}) async-start(f32[64,4,8,512]{3,2,1,0:T(8,128)} %bitcast.6), calls=%async_computation | async-start | bytes 8388608 | tf_op jit(solution)/shard_map/all_to_all | solution.py:353
  121.3 3.8 %collective-permute-start = (f32[256,512]{1,0:T(8,128)}, f32[256,512]{1,0:T(8,128)S(1)}, u32[]{:S(2)}, u32[]{:S(2)}) collective-permute-start(f32[256,512]{1,0:T(8,128)} %get-tuple-element.5), channel_id=1, source_target_pairs={{0,4},{4,0},{1,5},{5,1},{2,6},{6,2},{3,7},{7,3},{8,12},{12,8},{9,1... | collective-permute-start | bytes 1572872 | tf_op jit(solution)/shard_map/ppermute | solution.py:370
  168.3 5.4 %copy-start = (f32[16,16,512]{2,1,0:T(8,128)}, f32[16,16,512]{2,1,0:T(8,128)S(1)}, u32[]{:S(2)}) copy-start(f32[16,16,512]{2,1,0:T(8,128)S(1)} %all_to_all.22) | copy-start | bytes 1572868
  168.3 5.4 %collective-permute-start.1 = (f32[256,512]{1,0:T(8,128)S(1)}, f32[256,512]{1,0:T(8,128)S(1)}, u32[]{:S(2)}, u32[]{:S(2)}) collective-permute-start(f32[256,512]{1,0:T(8,128)S(1)} %bitcast.8), channel_id=1, source_target_pairs={{0,4},{4,0},{1,5},{5,1},{2,6},{6,2},{3,7},{7,3},{8,12},{12,8},{9,1... | collective-permute-start | bytes 1572872 | tf_op jit(solution)/shard_map/ppermute | solution.py:374
  173.8 0.8 copy-start.1
